TPU v7x, 32 devices: a whole 2x2x4 slice. The times are simulated.
32 devices in a mesh: cand: 2 (over x), expert: 16 (over z, y, core).
Axes of the slice: x: 2, y: 2, z: 4, core: 2. Of those that a mesh axis runs over, the one named last changes fastest.
Arguments:
- tokens: bfloat16 [2048, 2048], P('expert'), may hold values from -6 to 6
- targets: bfloat16 [2048, 2048], P('expert'), may hold values from -3 to 3
- routes: int32 [4096, 2], P(('cand', 'expert')), parts along dimension 0, may hold values from 0 to 3, all different within a row; in each aligned block of 128 rows (0 to 127, 128 to 255, ...) at most 80 rows name the same one
- gate_ints: int32 [4096, 2], P(('cand', 'expert')), parts along dimension 0, may hold values from 1 to 4096
- expert_home: int32 [8], P('cand'), parts along dimension 0, may hold values from 0 to 3, each once
- gate_up: bfloat16 [2, 8192, 2048], P(None, ('cand', 'expert')), parts along dimension 1, may hold values from -0.125 to 0.125
- down_master: float32 [8192, 2048], P(('cand', 'expert')), parts along dimension 0, may hold values from -0.1875 to 0.1875
- moment1: float32 [8192, 2048], P(('cand', 'expert')), parts along dimension 0, may hold values from -3 to 3
- moment2: float32 [8192, 2048], P(('cand', 'expert')), parts along dimension 0, may hold values from 0.005 to 0.05
Outputs:
- step_taken: float32 [8192, 2048], P(('cand', 'expert')), parts along dimension 0
- moment1_new: float32 [8192, 2048], P(('cand', 'expert')), parts along dimension 0
There are 2 independent parts, one for each index of `cand`. A program takes and returns all parts, laid end to end along the dimension named above; an argument that names none is the same for every part. Nothing has to cross between parts.
Inputs may be any that keep to these rules, and one draw needn't show every extreme that they name: `routes`: each row names 2 different experts; among the rows of one device no expert is named more than 80 times, a bound that some block reaches. `expert_home`: a permutation of the experts.
All inputs are finite; a program needn't handle non-finite values.
Results may differ from a plain program's by a relative error of at most 0.007.
Values may be sent and summed in bfloat16 or wider, within the bound.
A program may use at most 128 MiB of HBM per device.

v0:
```python
import jax
import jax.numpy as jnp
from jax import lax
from jax.sharding import PartitionSpec as P

GROUP = 4


learn_rate = 0.02
epsilon = 1e-08
prior_steps = 20
loss_scale = 0.125


def swapped(block, axis, bit):
    count = lax.axis_size(axis)
    route = []
    for low in range(count):
        high = low | 1 << bit
        if high != low and high < count:
            route += [(low, high), (high, low)]
    return lax.ppermute(block, axis, route)


def adam_step(master, moment_one, moment_two, gradient, count):
    moment_one = 0.9 * moment_one + 0.1 * gradient
    moment_two = 0.999 * moment_two + 0.001 * gradient * gradient
    first_fix = 1.0 - 0.9 ** (prior_steps + count)
    second_fix = 1.0 - 0.999 ** (prior_steps + count)
    master = master - learn_rate * (moment_one / first_fix) / (
        jnp.sqrt(moment_two / second_fix) + epsilon
    )
    return (master, moment_one, moment_two)


def member_gather(segment, member):
    for bit_index in range(GROUP.bit_length() - 1):
        partner_part = swapped(segment, "expert", bit_index)
        upper_bit = member >> bit_index & 1
        segment = jnp.where(
            upper_bit == 1,
            jnp.concatenate([partner_part, segment], axis=2),
            jnp.concatenate([segment, partner_part], axis=2),
        )
    return segment


def slices_out(outgoing, member):
    groups, members, capacity, slice_width = outgoing.shape
    received = lax.all_to_all(
        outgoing.reshape(groups * members, capacity, slice_width),
        "expert",
        split_axis=0,
        concat_axis=0,
        tiled=True,
    )
    return member_gather(received, member).reshape(-1, slice_width * members)


def split_pieces(pieces, member, bit_index):
    half_width = pieces.shape[2] // 2
    upper_bit = member >> bit_index & 1
    kept_part = jnp.where(upper_bit == 1, pieces[:, :, half_width:], pieces[:, :, :half_width])
    given_part = jnp.where(upper_bit == 1, pieces[:, :, :half_width], pieces[:, :, half_width:])
    return (kept_part, given_part)


def member_reduce(partial_value, member):
    top_bit = GROUP.bit_length() - 2
    kept_part, given_part = split_pieces(partial_value[None], member, top_bit)
    pieces = jnp.concatenate([kept_part, swapped(given_part, "expert", top_bit)], axis=0)
    kept_part, given_part = split_pieces(pieces, member, 0)
    pieces = jnp.concatenate([kept_part, swapped(given_part, "expert", 0)], axis=0)
    return jnp.sum(pieces.astype(jnp.float32), axis=0)


def shards(tokens, targets, routes, gate_ints, expert_home, gate_up, down_master, moment1, moment2):
    devices = lax.axis_size("expert")
    member = lax.axis_index("expert") % GROUP
    tok_rows, top_count = routes.shape
    feat_width = tokens.shape[1]
    groups = devices // GROUP
    experts = expert_home.shape[0]
    capacity = (5 * tok_rows * top_count * GROUP + 4 * devices - 1) // (4 * devices)
    slot_rows = groups * capacity
    flat_ids = routes.reshape(-1)
    onehot = (flat_ids[:, None] == jnp.arange(experts, dtype=jnp.int32)[None, :]).astype(jnp.int32)
    slot_rank = jnp.sum((jnp.cumsum(onehot, axis=0) - onehot) * onehot, axis=1)
    slot_home = jnp.sum(onehot * expert_home[None, :], axis=1)
    slot_dest = slot_home * capacity + slot_rank
    placed = jnp.arange(slot_rows, dtype=jnp.int32)[:, None] == slot_dest[None, :]
    weights = gate_ints.reshape(-1).astype(jnp.float32) / 4096.0
    pick_matrix = jnp.sum(
        placed.astype(jnp.float32).reshape(slot_rows, tok_rows, top_count), axis=2
    ).astype(jnp.bfloat16)
    mixing = jnp.sum(
        jnp.where(placed, weights[None, :], 0.0).reshape(slot_rows, tok_rows, top_count), axis=2
    )
    mixing_blocks = mixing.reshape(groups, capacity, tok_rows)
    highest = lax.Precision.HIGHEST
    segments = tokens.reshape(tok_rows, GROUP, feat_width // GROUP)
    outgoing = jnp.einsum(
        "gpt,tjc->gjpc",
        pick_matrix.reshape(groups, capacity, tok_rows),
        segments,
        preferred_element_type=jnp.float32,
    ).astype(jnp.bfloat16)
    arrived = slices_out(outgoing, member)
    gate_acts = lax.dot_general(
        arrived, gate_up[0], (((1,), (1,)), ((), ())), preferred_element_type=jnp.float32
    )
    up_acts = lax.dot_general(
        arrived, gate_up[1], (((1,), (1,)), ((), ())), preferred_element_type=jnp.float32
    )
    hidden = (jax.nn.silu(gate_acts) * up_acts).astype(jnp.bfloat16)
    target_values = targets.astype(jnp.float32)
    master, moment_one, moment_two = (down_master, moment1, moment2)
    for round_index in range(2):
        partial_value = jnp.dot(
            hidden, master.astype(jnp.bfloat16), preferred_element_type=jnp.float32
        ).astype(jnp.bfloat16)
        reduced = member_reduce(partial_value, member)
        returned = lax.all_to_all(
            reduced.reshape(devices, capacity, feat_width // GROUP),
            "expert",
            split_axis=0,
            concat_axis=0,
            tiled=True,
        )
        mixed = jnp.einsum(
            "gpt,gjpc->tjc",
            mixing_blocks,
            returned.reshape(groups, GROUP, capacity, feat_width // GROUP),
            precision=highest,
            preferred_element_type=jnp.float32,
        ).reshape(tok_rows, feat_width)
        residual = (mixed - target_values) * loss_scale
        grads_out = jnp.einsum(
            "gpt,tjc->gjpc",
            mixing_blocks,
            residual.reshape(tok_rows, GROUP, feat_width // GROUP),
            precision=highest,
            preferred_element_type=jnp.float32,
        ).astype(jnp.bfloat16)
        grad_rows = slices_out(grads_out, member)
        gradient = lax.dot_general(
            hidden, grad_rows, (((0,), (0,)), ((), ())), preferred_element_type=jnp.float32
        )
        master, moment_one, moment_two = adam_step(
            master, moment_one, moment_two, gradient, round_index + 1
        )
    return ((down_master - master) / learn_rate, moment_one)


def solution(mesh):
    in_specs = (
        P("expert", None),
        P("expert", None),
        P(("cand", "expert"), None),
        P(("cand", "expert"), None),
        P("cand"),
        P(None, ("cand", "expert"), None),
        P(("cand", "expert"), None),
        P(("cand", "expert"), None),
        P(("cand", "expert"), None),
    )
    out_specs = (P(("cand", "expert"), None), P(("cand", "expert"), None))
    return jax.shard_map(shards, mesh=mesh, in_specs=in_specs, out_specs=out_specs, check_vma=False)
```

profile of v0, /device:TPU:11, one launch (start us, length us, event | category | flops | bytes accessed | tf_op | source)
XLA Modules:
  0.0 599.2 jit_solution(5368091650584189073)
XLA Ops:
  2.4 1.2 reduce-window.6
  5.0 1.5 convolution_convert_fusion.4
  6.6 37.5 %all_to_all.25 = bf16[16,80,512]{2,1,0:T(8,128)(2,1)S(1)} all-to-all(bf16[16,80,512]{2,1,0:T(8,128)(2,1)S(1)} %bitcast.110), channel_id=1, replica_groups=mesh['cand'=2,'expert'=16] {'expert'}, dimensions={0} | all-to-all | bytes 2621440 | tf_op jit(solution)/shard_map/all_to_all | solution.py:50
  44.1 3.0 collective-permute-done
  47.1 1.9 maximum_select_fusion.5
  50.3 57.4 %collective-permute-done.1 = bf16[16,80,1024]{2,1,0:T(8,128)(2,1)} collective-permute-done((bf16[16,80,1024]{2,1,0:T(8,128)(2,1)}, bf16[16,80,1024]{2,1,0:T(8,128)(2,1)}, u32[]{:S(2)}, u32[]{:S(2)}) %collective-permute-start.1) | collective-permute-done | bytes 2621472 | tf_op jit(solution)/shard_map/ppermute | solution.py:22
  107.6 4.2 fusion.39
  111.9 4.5 multiply_convert_fusion
  116.4 1.5 fusion
  118.8 57.0 %collective-permute-done.2 = bf16[1,1280,1024]{2,1,0:T(8,128)(2,1)S(1)} collective-permute-done((bf16[1,1280,1024]{2,1,0:T(8,128)(2,1)S(1)}, bf16[1,1280,1024]{2,1,0:T(8,128)(2,1)S(1)}, u32[]{:S(2)}, u32[]{:S(2)}) %collective-permute-start.2) | collective-permute-done | bytes 2621472 | tf_op jit(solution)/shard_map/ppermute | solution.py:22
  175.8 1.5 broadcast_select_fusion.7
  177.4 1.9 collective-permute-start.3
  179.3 4.5 collective-permute-done.3
  184.7 63.3 %all_to_all.26 = f32[16,80,512]{2,1,0:T(8,128)S(1)} all-to-all(f32[16,80,512]{2,1,0:T(8,128)S(1)} %bitcast.108), channel_id=1, replica_groups=mesh['cand'=2,'expert'=16] {'expert'}, dimensions={0} | all-to-all | bytes 5242880 | tf_op jit(solution)/shard_map/all_to_all | solution.py:123
  249.0 2.0 fusion.19
  251.8 2.4 fusion.31
  254.3 35.5 %all_to_all.27 = bf16[16,80,512]{2,1,0:T(8,128)(2,1)S(1)} all-to-all(bf16[16,80,512]{2,1,0:T(8,128)(2,1)S(1)} %bitcast.111), channel_id=1, replica_groups=mesh['cand'=2,'expert'=16] {'expert'}, dimensions={0} | all-to-all | bytes 2621440 | tf_op jit(solution)/shard_map/all_to_all | solution.py:50
  289.8 3.0 collective-permute-done.4
  295.0 57.0 %collective-permute-done.5 = bf16[16,80,1024]{2,1,0:T(8,128)(2,1)S(1)} collective-permute-done((bf16[16,80,1024]{2,1,0:T(8,128)(2,1)S(1)}, bf16[16,80,1024]{2,1,0:T(8,128)(2,1)S(1)}, u32[]{:S(2)}, u32[]{:S(2)}) %collective-permute-start.5) | collective-permute-done | bytes 2621472 | tf_op jit(solution)/shard_map/ppermute | solution.py:22
  352.0 1.8 fusion.2
  354.9 2.4 fusion.1
  358.2 57.0 %collective-permute-done.6 = bf16[1,1280,1024]{2,1,0:T(8,128)(2,1)S(1)} collective-permute-done((bf16[1,1280,1024]{2,1,0:T(8,128)(2,1)S(1)}, bf16[1,1280,1024]{2,1,0:T(8,128)(2,1)S(1)}, u32[]{:S(2)}, u32[]{:S(2)}) %collective-permute-start.6) | collective-permute-done | bytes 2621472 | tf_op jit(solution)/shard_map/ppermute | solution.py:22
  415.1 1.5 broadcast_select_fusion.5
  416.7 1.9 collective-permute-start.7
  418.6 4.5 collective-permute-done.7
  424.0 63.3 %all_to_all.28 = f32[16,80,512]{2,1,0:T(8,128)S(1)} all-to-all(f32[16,80,512]{2,1,0:T(8,128)S(1)} %bitcast.109), channel_id=1, replica_groups=mesh['cand'=2,'expert'=16] {'expert'}, dimensions={0} | all-to-all | bytes 5242880 | tf_op jit(solution)/shard_map/all_to_all | solution.py:123
  487.6 2.0 fusion.21
  490.4 2.4 fusion.32
  492.9 35.5 %all_to_all.29 = bf16[16,80,512]{2,1,0:T(8,128)(2,1)S(1)} all-to-all(bf16[16,80,512]{2,1,0:T(8,128)(2,1)S(1)} %bitcast.112), channel_id=1, replica_groups=mesh['cand'=2,'expert'=16] {'expert'}, dimensions={0} | all-to-all | bytes 2621440 | tf_op jit(solution)/shard_map/all_to_all | solution.py:50
  528.4 3.0 collective-permute-done.8
  533.6 57.0 %collective-permute-done.9 = bf16[16,80,1024]{2,1,0:T(8,128)(2,1)S(1)} collective-permute-done((bf16[16,80,1024]{2,1,0:T(8,128)(2,1)S(1)}, bf16[16,80,1024]{2,1,0:T(8,128)(2,1)S(1)}, u32[]{:S(2)}, u32[]{:S(2)}) %collective-permute-start.9) | collective-permute-done | bytes 2621472 | tf_op jit(solution)/shard_map/ppermute | solution.py:22
  590.6 8.5 %fusion.30 = (f32[256,2048]{1,0:T(8,128)}, f32[256,2048]{1,0:T(8,128)}) fusion(f32[256,2048]{1,0:T(8,128)S(1)} %copy-done.3, f32[256,2048]{1,0:T(8,128)S(1)} %copy-done.10, f32[256,2048]{1,0:T(8,128)S(1)} %copy-done.6, f32[256,2048]{1,0:T(8,128)S(1)} %copy-done.8, bf16[1280,256]{1,0:T(8,128)(2,1)S(1)} %multiply_convert_fusion, ...), kind=kOutput, calls=%fused_computation.64 | convolution fusion | flops 1379401728 | bytes 18481152 | tf_op jit(solution)/shard_map/dot_general | solution.py:146
  (61 shorter events, 16.2 us)
Async XLA Ops:
  44.1 3.0 collective-permute-start
  49.0 58.6 %collective-permute-start.1 = (bf16[16,80,1024]{2,1,0:T(8,128)(2,1)}, bf16[16,80,1024]{2,1,0:T(8,128)(2,1)}, u32[]{:S(2)}, u32[]{:S(2)}) collective-permute-start(bf16[16,80,1024]{2,1,0:T(8,128)(2,1)} %maximum_select_fusion.5), channel_id=1, source_target_pairs={{0,2},{2,0},{1,3},{3,1},{4,6},{6,4},{5,7},{7,5},{8,10},{10,8},{9,1... | collective-permute-start | bytes 7864328 | tf_op jit(solution)/shard_map/ppermute | solution.py:22
  49.5 58.1 %copy-start.4 = (bf16[2,256,2048]{2,1,0:T(8,128)(2,1)S(1)}, bf16[2,256,2048]{2,1,0:T(8,128)(2,1)}, u32[]{:S(2)}) copy-start(bf16[2,256,2048]{2,1,0:T(8,128)(2,1)} %param.14) | copy-start | bytes 6291460
  111.9 4.6 copy-start.1
  118.3 57.5 %collective-permute-start.2 = (bf16[1,1280,1024]{2,1,0:T(8,128)(2,1)S(1)}, bf16[1,1280,1024]{2,1,0:T(8,128)(2,1)S(1)}, u32[]{:S(2)}, u32[]{:S(2)}) collective-permute-start(bf16[1,1280,1024]{2,1,0:T(8,128)(2,1)S(1)} %get-tuple-element.15), channel_id=1, source_target_pairs={{0,2},{2,0},{1,3},{3,1},{4,6},{6,4},{5,7},{7,5},{8,10},{10,8},{9,1... | collective-permute-start | bytes 7864328 | tf_op jit(solution)/shard_map/ppermute | solution.py:22
  177.4 6.5 %collective-permute-start.3 = (bf16[2,1280,512]{2,1,0:T(8,128)(2,1)S(1)}, bf16[2,1280,512]{2,1,0:T(8,128)(2,1)S(1)}, u32[]{:S(2)}, u32[]{:S(2)}) collective-permute-start(bf16[2,1280,512]{2,1,0:T(8,128)(2,1)S(1)} %get-tuple-element.13), channel_id=1, source_target_pairs={{0,1},{1,0},{2,3},{3,2},{4,5},{5,4},{6,7},{7,6},{8,9},{9,8},{10,11... | collective-permute-start | bytes 7864328 | tf_op jit(solution)/shard_map/ppermute | solution.py:22
  248.0 1.0 copy-start
  289.8 3.0 collective-permute-start.4
  293.7 58.4 %collective-permute-start.5 = (bf16[16,80,1024]{2,1,0:T(8,128)(2,1)S(1)}, bf16[16,80,1024]{2,1,0:T(8,128)(2,1)S(1)}, u32[]{:S(2)}, u32[]{:S(2)}) collective-permute-start(bf16[16,80,1024]{2,1,0:T(8,128)(2,1)S(1)} %maximum_select_fusion.7), channel_id=1, source_target_pairs={{0,2},{2,0},{1,3},{3,1},{4,6},{6,4},{5,7},{7,5},{8,10},{10,8},{9,1... | collective-permute-start | bytes 7864328 | tf_op jit(solution)/shard_map/ppermute | solution.py:22
  352.0 1.8 copy-start.2
  352.0 2.2 copy-start.5
  352.0 2.9 copy-start.7
  354.9 2.4 copy-start.9
  357.6 57.5 %collective-permute-start.6 = (bf16[1,1280,1024]{2,1,0:T(8,128)(2,1)S(1)}, bf16[1,1280,1024]{2,1,0:T(8,128)(2,1)S(1)}, u32[]{:S(2)}, u32[]{:S(2)}) collective-permute-start(bf16[1,1280,1024]{2,1,0:T(8,128)(2,1)S(1)} %get-tuple-element.11), channel_id=1, source_target_pairs={{0,2},{2,0},{1,3},{3,1},{4,6},{6,4},{5,7},{7,5},{8,10},{10,8},{9,1... | collective-permute-start | bytes 7864328 | tf_op jit(solution)/shard_map/ppermute | solution.py:22
  416.7 6.5 %collective-permute-start.7 = (bf16[2,1280,512]{2,1,0:T(8,128)(2,1)S(1)}, bf16[2,1280,512]{2,1,0:T(8,128)(2,1)S(1)}, u32[]{:S(2)}, u32[]{:S(2)}) collective-permute-start(bf16[2,1280,512]{2,1,0:T(8,128)(2,1)S(1)} %get-tuple-element.9), channel_id=1, source_target_pairs={{0,1},{1,0},{2,3},{3,2},{4,5},{5,4},{6,7},{7,6},{8,9},{9,8},{10,11... | collective-permute-start | bytes 7864328 | tf_op jit(solution)/shard_map/ppermute | solution.py:22
  528.4 3.0 collective-permute-start.8
  531.4 59.2 %copy-start.8 = (f32[256,2048]{1,0:T(8,128)S(1)}, f32[256,2048]{1,0:T(8,128)}, u32[]{:S(2)}) copy-start(f32[256,2048]{1,0:T(8,128)} %param.16) | copy-start | bytes 6291460
  531.4 59.2 %copy-start.10 = (f32[256,2048]{1,0:T(8,128)S(1)}, f32[256,2048]{1,0:T(8,128)}, u32[]{:S(2)}) copy-start(f32[256,2048]{1,0:T(8,128)} %copy-done.9) | copy-start | bytes 6291460
  532.3 58.4 %collective-permute-start.9 = (bf16[16,80,1024]{2,1,0:T(8,128)(2,1)S(1)}, bf16[16,80,1024]{2,1,0:T(8,128)(2,1)S(1)}, u32[]{:S(2)}, u32[]{:S(2)}) collective-permute-start(bf16[16,80,1024]{2,1,0:T(8,128)(2,1)S(1)} %maximum_select_fusion.9), channel_id=1, source_target_pairs={{0,2},{2,0},{1,3},{3,1},{4,6},{6,4},{5,7},{7,5},{8,10},{10,8},{9,1... | collective-permute-start | bytes 7864328 | tf_op jit(solution)/shard_map/ppermute | solution.py:22
  532.8 57.8 %copy-start.3 = (f32[256,2048]{1,0:T(8,128)S(1)}, f32[256,2048]{1,0:T(8,128)}, u32[]{:S(2)}) copy-start(f32[256,2048]{1,0:T(8,128)} %param.15) | copy-start | bytes 6291460
  532.8 57.8 %copy-start.6 = (f32[256,2048]{1,0:T(8,128)S(1)}, f32[256,2048]{1,0:T(8,128)}, u32[]{:S(2)}) copy-start(f32[256,2048]{1,0:T(8,128)} %param.17) | copy-start | bytes 6291460
where the time goes:
time: 602 us; the launch traced here: 599 us
  waiting for transfers between devices  304 us (50%)
  blocking collectives  235 us (39%)
  matrix products  33.4 us (6%)
  other arithmetic  14.2 us (2%)
  starting transfers between devices  6.39 us (1%)
    ppermute x10, waiting for transfers between devices, swapped(): return lax.ppermute(block, axis, route)  304 us
    all_to_all x2, blocking collectives, shards(): lax.all_to_all(reduced.reshape(devices, capacity, feat_width // GROUP), '...  127 us
    all_to_all x3, blocking collectives, slices_out(): lax.all_to_all(outgoing.reshape(groups * members, capacity, slice_width),...  108 us
  transfers between devices with their start and end apart: 10, of which 10 were waited for; matrix products, arithmetic and copies ran while one was open for 0% of the time, Pallas kernels for 0%

commit v1 on v0

v1 whole, which is shorter than its diff:
```python
import jax
import jax.numpy as jnp
from jax import lax
from jax.sharding import PartitionSpec as P

GROUP = 4


learn_rate = 0.02
epsilon = 1e-08
prior_steps = 20
loss_scale = 0.125


def flipped(block, mask):
    count = lax.axis_size("expert")
    return lax.ppermute(block, "expert", [(i, i ^ mask) for i in range(count)])


def member_gather(block, axis):
    across = flipped(block, 2)
    near = flipped(block, 1)
    far = flipped(across, 1)
    return jnp.concatenate([block, near, across, far], axis=axis)


def feature_slice(block, index, width):
    return lax.dynamic_slice_in_dim(block, index * width, width, axis=1)


def to_slices(block, member):
    width = block.shape[1] // GROUP
    pieces = [feature_slice(block, member, width)]
    for mask in range(1, GROUP):
        pieces.append(flipped(feature_slice(block, member ^ mask, width), mask))
    return jnp.stack(pieces)


def to_rows(block, member):
    pieces = [block[0]] + [flipped(block[mask], mask) for mask in range(1, GROUP)]
    for bit in range(GROUP.bit_length() - 1):
        upper = (member >> bit & 1) == 1
        step = 1 << bit
        pieces = [jnp.where(upper, pieces[i ^ step], pieces[i]) for i in range(GROUP)]
    return jnp.concatenate(pieces, axis=1)


def over_groups(block):
    groups = block.shape[0]
    lists = [[g * GROUP + m for g in range(groups)] for m in range(GROUP)]
    return lax.all_to_all(
        block, "expert", split_axis=0, concat_axis=0, tiled=True, axis_index_groups=lists
    )


def shards(tokens, targets, routes, gate_ints, expert_home, gate_up, down_master, moment1, moment2):
    devices = lax.axis_size("expert")
    member = lax.axis_index("expert") % GROUP
    tok_rows, top_count = routes.shape
    feat_width = tokens.shape[1]
    width = feat_width // GROUP
    groups = devices // GROUP
    experts = expert_home.shape[0]
    capacity = (5 * tok_rows * top_count * GROUP + 4 * devices - 1) // (4 * devices)
    slot_rows = groups * capacity
    bf16, f32 = jnp.bfloat16, jnp.float32

    flat_ids = routes.reshape(-1)
    onehot = (flat_ids[:, None] == jnp.arange(experts, dtype=jnp.int32)[None, :]).astype(jnp.int32)
    slot_rank = jnp.sum((jnp.cumsum(onehot, axis=0) - onehot) * onehot, axis=1)
    slot_home = jnp.sum(onehot * expert_home[None, :], axis=1)
    slot_dest = (slot_home * capacity + slot_rank).reshape(tok_rows, top_count)

    row_ids = jnp.arange(slot_rows, dtype=jnp.int32)
    pick_own = jnp.zeros((slot_rows, tok_rows), jnp.bool_)
    for k in range(top_count):
        pick_own = pick_own | (row_ids[:, None] == slot_dest[:, k][None, :])
    outgoing = jnp.dot(
        pick_own.astype(bf16), tokens, preferred_element_type=f32
    ).astype(bf16).reshape(groups, capacity, feat_width)

    plan = member_gather(
        jnp.stack([slot_dest.T, gate_ints.T], axis=1)[None], 0
    )
    all_dest, all_gates = plan[:, :, 0], plan[:, :, 1]
    weights = all_gates.astype(f32) / 4096.0
    picks = (all_dest[:, :, :, None] == row_ids).astype(bf16)

    arrived = member_gather(over_groups(outgoing), 1)
    rows = groups * GROUP * capacity
    arrived = arrived.reshape(rows, feat_width)

    master = to_slices(down_master.astype(bf16), member)
    goal = to_slices(targets, member)
    moment_one = to_slices(moment1.astype(bf16), member)
    moment_two = to_slices(moment2.astype(bf16), member)
    units = master.shape[1]
    flat = (GROUP * units, width)
    master = master.reshape(flat).astype(f32)
    moment_one = moment_one.reshape(flat).astype(f32)
    moment_two = moment_two.reshape(flat).astype(f32)
    goal = goal.astype(f32)

    gate_acts = lax.dot_general(
        arrived, gate_up[0], (((1,), (1,)), ((), ())), preferred_element_type=f32
    )
    up_acts = lax.dot_general(
        arrived, gate_up[1], (((1,), (1,)), ((), ())), preferred_element_type=f32
    )
    own_hidden = (jax.nn.silu(gate_acts) * up_acts).astype(bf16)
    across = flipped(own_hidden, 2)
    hiddens = [own_hidden, flipped(own_hidden, 1), across, flipped(across, 1)]
    hidden = jnp.concatenate(
        [
            jnp.stack(
                [block.reshape(groups, GROUP, capacity, -1)[:, i ^ mask] for i in range(GROUP)],
                axis=1,
            ).reshape(rows, -1)
            for mask, block in enumerate(hiddens)
        ],
        axis=1,
    )

    moved = jnp.zeros(flat, f32)
    for round_index in range(2):
        summed = jnp.dot(hidden, master.astype(bf16), preferred_element_type=f32).astype(bf16)
        returned = over_groups(summed.reshape(groups, GROUP, capacity, width))
        returned = returned.transpose(1, 0, 2, 3).reshape(GROUP, slot_rows, width)
        mixed = jnp.zeros((GROUP, tok_rows, width), f32)
        for k in range(top_count):
            picked = jnp.einsum(
                "mts,msc->mtc", picks[:, k], returned, preferred_element_type=f32
            )
            mixed = mixed + weights[:, k, :, None] * picked
        residual = (mixed - goal) * loss_scale
        slot_values = (weights[:, :, :, None] * residual[:, None]).astype(bf16)
        grads_out = jnp.einsum(
            "mks,mkc->msc",
            picks.reshape(GROUP, top_count * tok_rows, slot_rows),
            slot_values.reshape(GROUP, top_count * tok_rows, width),
            preferred_element_type=f32,
        ).astype(bf16)
        grads_out = grads_out.reshape(GROUP, groups, capacity, width).transpose(1, 0, 2, 3)
        grad_rows = over_groups(grads_out).reshape(rows, width)
        gradient = lax.dot_general(
            hidden, grad_rows, (((0,), (0,)), ((), ())), preferred_element_type=f32
        )
        count = round_index + 1
        moment_one = 0.9 * moment_one + 0.1 * gradient
        moment_two = 0.999 * moment_two + 0.001 * gradient * gradient
        first_fix = 1.0 - 0.9 ** (prior_steps + count)
        second_fix = 1.0 - 0.999 ** (prior_steps + count)
        change = (moment_one / first_fix) / (jnp.sqrt(moment_two / second_fix) + epsilon)
        moved = moved + change
        master = master - learn_rate * change
    shape = (GROUP, units, width)
    return (
        to_rows(moved.astype(bf16).reshape(shape), member).astype(f32),
        to_rows(moment_one.astype(bf16).reshape(shape), member).astype(f32),
    )


def solution(mesh):
    in_specs = (
        P("expert", None),
        P("expert", None),
        P(("cand", "expert"), None),
        P(("cand", "expert"), None),
        P("cand"),
        P(None, ("cand", "expert"), None),
        P(("cand", "expert"), None),
        P(("cand", "expert"), None),
        P(("cand", "expert"), None),
    )
    out_specs = (P(("cand", "expert"), None), P(("cand", "expert"), None))
    return jax.shard_map(shards, mesh=mesh, in_specs=in_specs, out_specs=out_specs, check_vma=False)
```

time: 602 us -> 315 us (0.52)
  waiting for transfers between devices: 304 us -> 106 us
  blocking collectives: 235 us -> 100 us
  starting transfers between devices: 6.39 us -> 40.8 us
  local copies, waits for them, and re-layouts: 5.61 us -> 20.9 us
  matrix products: 33.4 us -> 26.8 us
    ppermute x10 -> x27, waiting for transfers between devices: 304 us -> 84.4 us  [flipped(): return lax.ppermute(block, 'expert', [(i, i ^ mask) for i in range(count)])]
    all_to_all x5 -> x3, blocking collectives: 235 us -> 100 us  [over_groups(): lax.all_to_all(block, 'expert', split_axis=0, concat_axis=0, tiled=True,...]
    ppermute x10 -> x27, starting transfers between devices: 6.39 us -> 28 us  [flipped(): return lax.ppermute(block, 'expert', [(i, i ^ mask) for i in range(count)])]
    all_to_all x0 -> x2, waiting for transfers between devices: none -> 21.1 us  [over_groups(): lax.all_to_all(block, 'expert', split_axis=0, concat_axis=0, tiled=True,...]
    all_to_all x0 -> x2, starting transfers between devices: none -> 12.8 us  [over_groups(): lax.all_to_all(block, 'expert', split_axis=0, concat_axis=0, tiled=True,...]
    select_n x10 -> x2, other arithmetic: 9.66 us -> 2.32 us  [to_rows(): jnp.where(upper, pieces[i ^ step], pieces[i])]
    dot_general x7 -> x9, matrix products: 14.4 us -> 13.1 us  [the longest x2 7.5 us: shards(): jnp.dot(hidden, master.astype(bf16), preferred_element_type=f32)]
  transfers between devices with their start and end apart: 10 -> 29, of which waited for: 10 -> 14; matrix products, arithmetic and copies ran while one was open for 0% -> 7% of each run, Pallas kernels for 0% -> 0%
where the time goes in v1:
time: 315 us; the launch traced here: 312 us
  waiting for transfers between devices  106 us (34%)
  blocking collectives  100 us (32%)
  starting transfers between devices  40.8 us (13%)
  matrix products  26.8 us (9%)
  local copies, waits for them, and re-layouts  20.9 us (7%)
  other arithmetic  16.6 us (5%)
    all_to_all x3, blocking collectives, over_groups(): lax.all_to_all(block, 'expert', split_axis=0, concat_axis=0, tiled=True,...  100 us
    ppermute x27, waiting for transfers between devices, flipped(): return lax.ppermute(block, 'expert', [(i, i ^ mask) for i in range(count)])  84.4 us
    ppermute x27, starting transfers between devices, flipped(): return lax.ppermute(block, 'expert', [(i, i ^ mask) for i in range(count)])  28 us
    all_to_all x2, waiting for transfers between devices, over_groups(): lax.all_to_all(block, 'expert', split_axis=0, concat_axis=0, tiled=True,...  21.1 us
    all_to_all x2, starting transfers between devices, over_groups(): lax.all_to_all(block, 'expert', split_axis=0, concat_axis=0, tiled=True,...  12.8 us
    dot_general x2, matrix products, shards(): lax.dot_general(hidden, grad_rows, (((0,), (0,)), ((), ())), preferred_el...  9.61 us
    dot_general x2, matrix products, shards(): jnp.dot(hidden, master.astype(bf16), preferred_element_type=f32)  7.5 us
  transfers between devices with their start and end apart: 29, of which 14 were waited for; matrix products, arithmetic and copies ran while one was open for 7% of the time, Pallas kernels for 0%

profile of v1, /device:TPU:11, one launch (start us, length us, event | category | flops | bytes accessed | tf_op | source)
XLA Modules:
  0.0 311.9 jit_solution(11125764359925974805)
XLA Ops:
  5.0 33.2 %all_to_all.25 = bf16[4,80,2048]{2,1,0:T(8,128)(2,1)S(1)} all-to-all(bf16[4,80,2048]{2,1,0:T(8,128)(2,1)S(1)} %bitcast.136), channel_id=1, replica_groups={{0,4,8,12},{1,5,9,13},{2,6,10,14},{3,7,11,15},{16,20,24,28},{17,21,25,2..., dimensions={0} | all-to-all | bytes 2621440 | tf_op jit(solution)/shard_map/all_to_all | solution.py:51
  39.5 2.4 collective-permute-start.3
  41.8 24.6 %collective-permute-done.4 = bf16[4,80,2048]{2,1,0:T(8,128)(2,1)S(1)} collective-permute-done((bf16[4,80,2048]{2,1,0:T(8,128)(2,1)S(1)}, bf16[4,80,2048]{2,1,0:T(8,128)(2,1)S(1)}, u32[]{:S(2)}, u32[]{:S(2)}) %collective-permute-start.4) | collective-permute-done | bytes 1310752 | tf_op jit(solution)/shard_map/ppermute | solution.py:17
  66.4 3.0 collective-permute-start.5
  69.4 2.7 collective-permute-done.5
  72.1 6.0 %pad_maximum_fusion = bf16[4,320,2048]{2,1,0:T(8,128)(2,1)S(1)} fusion(bf16[4,80,2048]{2,1,0:T(8,128)(2,1)S(1)} %collective-permute-done.5, bf16[4,80,2048]{2,1,0:T(8,128)(2,1)S(1)} %collective-permute-done.4, bf16[4,80,2048]{2,1,0:T(8,128)(2,1)S(1)} %collective-permute-done.3, bf16[4,80,2048]{2,1,0:T(8,128)(2,1)S(1)} %all_to_all.25), kind=kLoop, calls=%fused_computation | loop fusion | flops 20971520 | bytes 10485760 | tf_op jit(solution)/shard_map/concatenate | solution.py:24
  79.6 2.6 multiply_convert_fusion
  86.3 18.2 %collective-permute-done.13 = bf16[256,512]{1,0:T(8,128)(2,1)S(1)} collective-permute-done((bf16[256,512]{1,0:T(8,128)(2,1)S(1)}, bf16[256,512]{1,0:T(8,128)(2,1)S(1)}, u32[]{:S(2)}, u32[]{:S(2)}) %collective-permute-start.13) | collective-permute-done | bytes 262176 | tf_op jit(solution)/shard_map/ppermute | solution.py:17
  104.6 5.9 %collective-permute-done.14 = bf16[256,512]{1,0:T(8,128)(2,1)S(1)} collective-permute-done((bf16[256,512]{1,0:T(8,128)(2,1)S(1)}, bf16[256,512]{1,0:T(8,128)(2,1)S(1)}, u32[]{:S(2)}, u32[]{:S(2)}) %collective-permute-start.14) | collective-permute-done | bytes 262176 | tf_op jit(solution)/shard_map/ppermute | solution.py:17
  117.0 4.1 %convolution_convert_fusion.1 = bf16[1280,512]{1,0:T(8,128)(2,1)} fusion(bf16[1024,512]{1,0:T(8,128)(2,1)S(1)} %bitcast.141, bf16[1280,256]{0,1:T(8,128)(2,1)S(1)} %copy.75, bf16[1280,256]{0,1:T(8,128)(2,1)} %copy.74, bf16[1280,256]{0,1:T(8,128)(2,1)S(1)} %copy.73, bf16[1280,256]{0,1:T(8,128)(2,1)} %multiply_convert_fusion), kind=kOutput, calls=%fused_computation.4 | convolution fusion | flops 1353318400 | bytes 4980736 | tf_op jit(solution)/shard_map/dot_general | solution.py:126
  121.2 5.5 %all-to-all-start.1 = ((bf16[4,4,80,512]{3,2,1,0:T(8,128)(2,1)}), bf16[4,4,80,512]{3,2,1,0:T(8,128)(2,1)S(1)}, u32[]{:S(2)}, u32[]{:S(2)}) async-start(bf16[4,4,80,512]{3,2,1,0:T(8,128)(2,1)} %bitcast.149), calls=%async_computation.1 | async-start | bytes 2621440 | tf_op jit(solution)/shard_map/all_to_all | solution.py:51
  133.7 21.1 %all-to-all-done.1 = bf16[4,4,80,512]{3,2,1,0:T(8,128)(2,1)S(1)} async-done(((bf16[4,4,80,512]{3,2,1,0:T(8,128)(2,1)}), bf16[4,4,80,512]{3,2,1,0:T(8,128)(2,1)S(1)}, u32[]{:S(2)}, u32[]{:S(2)}) %all-to-all-start.1) | async-done | bytes 1310752 | tf_op jit(solution)/shard_map/all_to_all | solution.py:51
  158.8 7.2 %all-to-all-start.2 = ((bf16[4,4,80,512]{3,2,1,0:T(8,128)(2,1)}), bf16[4,4,80,512]{3,2,1,0:T(8,128)(2,1)}, u32[]{:S(2)}, u32[]{:S(2)}) async-start(bf16[4,4,80,512]{3,2,1,0:T(8,128)(2,1)} %bitcast.126), calls=%async_computation.2 | async-start | bytes 2621440 | tf_op jit(solution)/shard_map/all_to_all | solution.py:51
  166.1 1.9 convert_element_type.95
  168.1 1.6 collective-permute-start.18
  175.9 1.6 collective-permute-done.19
  177.6 6.7 %collective-permute-done.20 = bf16[256,512]{1,0:T(8,128)(2,1)S(1)} collective-permute-done((bf16[256,512]{1,0:T(8,128)(2,1)S(1)}, bf16[256,512]{1,0:T(8,128)(2,1)S(1)}, u32[]{:S(2)}, u32[]{:S(2)}) %collective-permute-start.20) | collective-permute-done | bytes 262176 | tf_op jit(solution)/shard_map/ppermute | solution.py:17
  186.3 1.8 copy.91
  188.8 5.9 %collective-permute-done.2 = bf16[256,512]{1,0:T(8,128)(2,1)} collective-permute-done((bf16[256,512]{1,0:T(8,128)(2,1)S(1)}, bf16[256,512]{1,0:T(8,128)(2,1)}, u32[]{:S(2)}, u32[]{:S(2)}) %collective-permute-start.2) | collective-permute-done | bytes 262176 | tf_op jit(solution)/shard_map/ppermute | solution.py:17
  196.1 1.8 copy.89
  197.9 4.7 %fusion.48 = f32[1024,512]{0,1:T(8,128)S(1)} fusion(bf16[1280,512]{1,0:T(8,128)(2,1)} %bitcast.49, bf16[1280,256]{0,1:T(8,128)(2,1)} %copy-done.11, bf16[1280,256]{0,1:T(8,128)(2,1)} %copy.74, bf16[1280,256]{0,1:T(8,128)(2,1)S(1)} %copy-done.8, bf16[1280,256]{0,1:T(8,128)(2,1)} %multiply_convert_fusion), kind=kOutput, calls=%fused_computation.128 | convolution fusion | flops 1352663040 | bytes 6029312 | tf_op jit(solution)/shard_map/dot_general | solution.py:145
  202.6 3.4 %convolution_convert_fusion = bf16[1280,512]{1,0:T(8,128)(2,1)S(1)} fusion(bf16[1024,512]{0,1:T(8,128)(2,1)S(1)} %copy-done.6, f32[1024,512]{0,1:T(8,128)S(1)} %copy-done.4, f32[1024,512]{0,1:T(8,128)S(1)} %fusion.48, f32[1024,512]{0,1:T(8,128)S(1)} %copy-done.5, bf16[1280,256]{0,1:T(8,128)(2,1)S(1)} %copy-done.12, bf16[1280,256]{0,1:T(8,128)(2,1)S(1)} %copy-done.10, ...), kind=kOutput, calls=%fused_computation.3 | convolution fusion | flops 1360134144 | bytes 11272192 | tf_op jit(solution)/shard_map/dot_general | solution.py:126
  206.0 33.8 %all_to_all.26 = bf16[4,4,80,512]{3,2,1,0:T(8,128)(2,1)S(1)} all-to-all(bf16[4,4,80,512]{3,2,1,0:T(8,128)(2,1)S(1)} %bitcast.151), channel_id=1, replica_groups={{0,4,8,12},{1,5,9,13},{2,6,10,14},{3,7,11,15},{16,20,24,28},{17,21,25,2..., dimensions={0} | all-to-all | bytes 2621440 | tf_op jit(solution)/shard_map/all_to_all | solution.py:51
  243.2 32.9 %all_to_all.27 = bf16[4,4,80,512]{3,2,1,0:T(8,128)(2,1)S(1)} all-to-all(bf16[4,4,80,512]{3,2,1,0:T(8,128)(2,1)S(1)} %bitcast.140), channel_id=1, replica_groups={{0,4,8,12},{1,5,9,13},{2,6,10,14},{3,7,11,15},{16,20,24,28},{17,21,25,2..., dimensions={0} | all-to-all | bytes 2621440 | tf_op jit(solution)/shard_map/all_to_all | solution.py:51
  276.1 5.0 %fusion.10 = (bf16[1024,512]{0,1:T(8,128)(2,1)S(1)}, bf16[1024,512]{0,1:T(8,128)(2,1)S(1)}) fusion(f32[1024,512]{0,1:T(8,128)S(1)} %copy-done.5, f32[1024,512]{0,1:T(8,128)S(1)} %fusion.48, f32[1024,512]{0,1:T(8,128)S(1)} %copy-done.4, bf16[1280,512]{1,0:T(8,128)(2,1)S(1)} %bitcast.150, bf16[1280,256]{0,1:T(8,128)(2,1)S(1)} %copy-done.12, ...), kind=kOutput, calls=%fused_computation.25 | convolution fusion | flops 1364721664 | bytes 12320768 | tf_op jit(solution)/shard_map/dot_general | solution.py:145
  281.2 3.4 %collective-permute-start.24 = (bf16[256,512]{0,1:T(8,128)(2,1)S(1)}, bf16[256,512]{0,1:T(8,128)(2,1)S(1)}, u32[]{:S(2)}, u32[]{:S(2)}) collective-permute-start(bf16[256,512]{0,1:T(8,128)(2,1)S(1)} %get-tuple-element.26), channel_id=1, source_target_pairs={{0,3},{1,2},{2,1},{3,0},{4,7},{5,6},{6,5},{7,4},{8,11},{9,10},{10,... | collective-permute-start | bytes 786440 | tf_op jit(solution)/shard_map/ppermute | solution.py:17
  287.6 4.1 %collective-permute-done.24 = bf16[256,512]{0,1:T(8,128)(2,1)S(1)} collective-permute-done((bf16[256,512]{0,1:T(8,128)(2,1)S(1)}, bf16[256,512]{0,1:T(8,128)(2,1)S(1)}, u32[]{:S(2)}, u32[]{:S(2)}) %collective-permute-start.24) | collective-permute-done | bytes 262176 | tf_op jit(solution)/shard_map/ppermute | solution.py:17
  292.1 5.3 %collective-permute-done.25 = bf16[256,512]{0,1:T(8,128)(2,1)} collective-permute-done((bf16[256,512]{0,1:T(8,128)(2,1)S(1)}, bf16[256,512]{0,1:T(8,128)(2,1)}, u32[]{:S(2)}, u32[]{:S(2)}) %collective-permute-start.25) | collective-permute-done | bytes 262176 | tf_op jit(solution)/shard_map/ppermute | solution.py:17
  298.7 1.8 copy.88
  300.5 2.5 collective-permute-done.21
  303.0 5.6 %collective-permute-done.22 = bf16[256,512]{0,1:T(8,128)(2,1)} collective-permute-done((bf16[256,512]{0,1:T(8,128)(2,1)}, bf16[256,512]{0,1:T(8,128)(2,1)}, u32[]{:S(2)}, u32[]{:S(2)}) %collective-permute-start.22) | collective-permute-done | bytes 262176 | tf_op jit(solution)/shard_map/ppermute | solution.py:17
  310.0 1.8 copy.87
  (150 shorter events, 48.3 us)
Async XLA Ops:
  38.2 39.8 %copy-start.20 = (bf16[2,256,2048]{2,1,0:T(8,128)(2,1)S(1)}, bf16[2,256,2048]{2,1,0:T(8,128)(2,1)}, u32[]{:S(2)}) copy-start(bf16[2,256,2048]{2,1,0:T(8,128)(2,1)} %param.14) | copy-start | bytes 6291460
  38.2 28.2 %collective-permute-start.4 = (bf16[4,80,2048]{2,1,0:T(8,128)(2,1)S(1)}, bf16[4,80,2048]{2,1,0:T(8,128)(2,1)S(1)}, u32[]{:S(2)}, u32[]{:S(2)}) collective-permute-start(bf16[4,80,2048]{2,1,0:T(8,128)(2,1)S(1)} %all_to_all.25), channel_id=1, source_target_pairs={{0,2},{1,3},{2,0},{3,1},{4,6},{5,7},{6,4},{7,5},{8,10},{9,11},{10,... | collective-permute-start | bytes 3932168 | tf_op jit(solution)/shard_map/ppermute | solution.py:17
  39.5 30.0 %collective-permute-start.3 = (bf16[4,80,2048]{2,1,0:T(8,128)(2,1)S(1)}, bf16[4,80,2048]{2,1,0:T(8,128)(2,1)S(1)}, u32[]{:S(2)}, u32[]{:S(2)}) collective-permute-start(bf16[4,80,2048]{2,1,0:T(8,128)(2,1)S(1)} %all_to_all.25), channel_id=1, source_target_pairs={{0,1},{1,0},{2,3},{3,2},{4,5},{5,4},{6,7},{7,6},{8,9},{9,8},{10,11... | collective-permute-start | bytes 3932168 | tf_op jit(solution)/shard_map/ppermute | solution.py:17
  66.4 5.6 %collective-permute-start.5 = (bf16[4,80,2048]{2,1,0:T(8,128)(2,1)S(1)}, bf16[4,80,2048]{2,1,0:T(8,128)(2,1)S(1)}, u32[]{:S(2)}, u32[]{:S(2)}) collective-permute-start(bf16[4,80,2048]{2,1,0:T(8,128)(2,1)S(1)} %collective-permute-done.4), channel_id=1, source_target_pairs={{0,1},{1,0},{2,3},{3,2},{4,5},{5,4},{6,7},{7,6},{8,9},{9,8},{10,11... | collective-permute-start | bytes 3932168 | tf_op jit(solution)/shard_map/ppermute | solution.py:17
  82.2 28.4 %collective-permute-start.6 = (bf16[1280,256]{0,1:T(8,128)(2,1)}, bf16[1280,256]{0,1:T(8,128)(2,1)}, u32[]{:S(2)}, u32[]{:S(2)}) collective-permute-start(bf16[1280,256]{0,1:T(8,128)(2,1)} %multiply_convert_fusion), channel_id=1, source_target_pairs={{0,1},{1,0},{2,3},{3,2},{4,5},{5,4},{6,7},{7,6},{8,9},{9,8},{10,11... | collective-permute-start | bytes 1966088 | tf_op jit(solution)/shard_map/ppermute | solution.py:17
  82.6 29.4 %collective-permute-start.7 = (bf16[1280,256]{0,1:T(8,128)(2,1)}, bf16[1280,256]{0,1:T(8,128)(2,1)}, u32[]{:S(2)}, u32[]{:S(2)}) collective-permute-start(bf16[1280,256]{0,1:T(8,128)(2,1)} %multiply_convert_fusion), channel_id=1, source_target_pairs={{0,2},{1,3},{2,0},{3,1},{4,6},{5,7},{6,4},{7,5},{8,10},{9,11},{10,... | collective-permute-start | bytes 1966088 | tf_op jit(solution)/shard_map/ppermute | solution.py:17
  84.1 2.2 collective-permute-start.12
  84.6 20.0 %collective-permute-start.13 = (bf16[256,512]{1,0:T(8,128)(2,1)S(1)}, bf16[256,512]{1,0:T(8,128)(2,1)S(1)}, u32[]{:S(2)}, u32[]{:S(2)}) collective-permute-start(bf16[256,512]{1,0:T(8,128)(2,1)S(1)} %get-tuple-element.40), channel_id=1, source_target_pairs={{0,2},{1,3},{2,0},{3,1},{4,6},{5,7},{6,4},{7,5},{8,10},{9,11},{10,... | collective-permute-start | bytes 786440 | tf_op jit(solution)/shard_map/ppermute | solution.py:17
  84.8 25.7 %collective-permute-start.14 = (bf16[256,512]{1,0:T(8,128)(2,1)S(1)}, bf16[256,512]{1,0:T(8,128)(2,1)S(1)}, u32[]{:S(2)}, u32[]{:S(2)}) collective-permute-start(bf16[256,512]{1,0:T(8,128)(2,1)S(1)} %get-tuple-element.39), channel_id=1, source_target_pairs={{0,3},{1,2},{2,1},{3,0},{4,7},{5,6},{6,5},{7,4},{8,11},{9,10},{10,... | collective-permute-start | bytes 786440 | tf_op jit(solution)/shard_map/ppermute | solution.py:17
  112.0 3.3 %collective-permute-start.8 = (bf16[1280,256]{0,1:T(8,128)(2,1)}, bf16[1280,256]{0,1:T(8,128)(2,1)}, u32[]{:S(2)}, u32[]{:S(2)}) collective-permute-start(bf16[1280,256]{0,1:T(8,128)(2,1)} %collective-permute-done.7), channel_id=1, source_target_pairs={{0,1},{1,0},{2,3},{3,2},{4,5},{5,4},{6,7},{7,6},{8,9},{9,8},{10,11... | collective-permute-start | bytes 1966088 | tf_op jit(solution)/shard_map/ppermute | solution.py:17
  121.2 33.6 %all-to-all-start.1 = ((bf16[4,4,80,512]{3,2,1,0:T(8,128)(2,1)}), bf16[4,4,80,512]{3,2,1,0:T(8,128)(2,1)S(1)}, u32[]{:S(2)}, u32[]{:S(2)}) async-start(bf16[4,4,80,512]{3,2,1,0:T(8,128)(2,1)} %bitcast.149), calls=%async_computation.1 | async-start | bytes 2621440 | tf_op jit(solution)/shard_map/all_to_all | solution.py:51
  126.8 2.8 collective-permute-start.10
  128.1 5.3 %collective-permute-start.9 = (s32[1,2,2,128]{3,2,1,0:T(2,128)S(1)}, s32[1,2,2,128]{3,2,1,0:T(2,128)S(1)}, u32[]{:S(2)}, u32[]{:S(2)}) collective-permute-start(s32[1,2,2,128]{3,2,1,0:T(2,128)S(1)} %get-tuple-element.63), channel_id=1, source_target_pairs={{0,1},{1,0},{2,3},{3,2},{4,5},{5,4},{6,7},{7,6},{8,9},{9,8},{10,11... | collective-permute-start | bytes 6152 | tf_op jit(solution)/shard_map/ppermute | solution.py:17
  129.6 3.8 %collective-permute-start.11 = (s32[1,2,2,128]{3,2,1,0:T(2,128)S(1)}, s32[1,2,2,128]{3,2,1,0:T(2,128)S(1)}, u32[]{:S(2)}, u32[]{:S(2)}) collective-permute-start(s32[1,2,2,128]{3,2,1,0:T(2,128)S(1)} %collective-permute-done.10), channel_id=1, source_target_pairs={{0,1},{1,0},{2,3},{3,2},{4,5},{5,4},{6,7},{7,6},{8,9},{9,8},{10,11... | collective-permute-start | bytes 6152 | tf_op jit(solution)/shard_map/ppermute | solution.py:17
  131.2 24.2 %copy-start.17 = (bf16[1,128,512]{2,1,0:T(8,128)(2,1)}, bf16[1,128,512]{2,1,0:T(8,128)(2,1)S(1)}, u32[]{:S(2)}) copy-start(bf16[1,128,512]{2,1,0:T(8,128)(2,1)S(1)} %get-tuple-element.52) | copy-start | bytes 393220
  131.2 24.2 %collective-permute-start.15 = (bf16[128,512]{1,0:T(8,128)(2,1)S(1)}, bf16[128,512]{1,0:T(8,128)(2,1)S(1)}, u32[]{:S(2)}, u32[]{:S(2)}) collective-permute-start(bf16[128,512]{1,0:T(8,128)(2,1)S(1)} %get-tuple-element.53), channel_id=1, source_target_pairs={{0,1},{1,0},{2,3},{3,2},{4,5},{5,4},{6,7},{7,6},{8,9},{9,8},{10,11... | collective-permute-start | bytes 393224 | tf_op jit(solution)/shard_map/ppermute | solution.py:17
  131.3 24.1 %collective-permute-start.16 = (bf16[128,512]{1,0:T(8,128)(2,1)S(1)}, bf16[128,512]{1,0:T(8,128)(2,1)}, u32[]{:S(2)}, u32[]{:S(2)}) collective-permute-start(bf16[128,512]{1,0:T(8,128)(2,1)S(1)} %get-tuple-element.55), channel_id=1, source_target_pairs={{0,2},{1,3},{2,0},{3,1},{4,6},{5,7},{6,4},{7,5},{8,10},{9,11},{10,... | collective-permute-start | bytes 393224 | tf_op jit(solution)/shard_map/ppermute | solution.py:17
  132.6 22.8 %collective-permute-start.17 = (bf16[128,512]{1,0:T(8,128)(2,1)S(1)}, bf16[128,512]{1,0:T(8,128)(2,1)}, u32[]{:S(2)}, u32[]{:S(2)}) collective-permute-start(bf16[128,512]{1,0:T(8,128)(2,1)S(1)} %get-tuple-element.54), channel_id=1, source_target_pairs={{0,3},{1,2},{2,1},{3,0},{4,7},{5,6},{6,5},{7,4},{8,11},{9,10},{10,... | collective-permute-start | bytes 393224 | tf_op jit(solution)/shard_map/ppermute | solution.py:17
  158.8 39.1 %all-to-all-start.2 = ((bf16[4,4,80,512]{3,2,1,0:T(8,128)(2,1)}), bf16[4,4,80,512]{3,2,1,0:T(8,128)(2,1)}, u32[]{:S(2)}, u32[]{:S(2)}) async-start(bf16[4,4,80,512]{3,2,1,0:T(8,128)(2,1)} %bitcast.126), calls=%async_computation.2 | async-start | bytes 2621440 | tf_op jit(solution)/shard_map/all_to_all | solution.py:51
  168.1 5.8 %collective-permute-start.18 = (bf16[256,512]{1,0:T(8,128)(2,1)S(1)}, bf16[256,512]{1,0:T(8,128)(2,1)S(1)}, u32[]{:S(2)}, u32[]{:S(2)}) collective-permute-start(bf16[256,512]{1,0:T(8,128)(2,1)S(1)} %get-tuple-element.37), channel_id=1, source_target_pairs={{0,1},{1,0},{2,3},{3,2},{4,5},{5,4},{6,7},{7,6},{8,9},{9,8},{10,11... | collective-permute-start | bytes 786440 | tf_op jit(solution)/shard_map/ppermute | solution.py:17
  169.7 7.9 %collective-permute-start.19 = (bf16[256,512]{1,0:T(8,128)(2,1)S(1)}, bf16[256,512]{1,0:T(8,128)(2,1)S(1)}, u32[]{:S(2)}, u32[]{:S(2)}) collective-permute-start(bf16[256,512]{1,0:T(8,128)(2,1)S(1)} %get-tuple-element.36), channel_id=1, source_target_pairs={{0,2},{1,3},{2,0},{3,1},{4,6},{5,7},{6,4},{7,5},{8,10},{9,11},{10,... | collective-permute-start | bytes 786440 | tf_op jit(solution)/shard_map/ppermute | solution.py:17
  170.9 13.4 %collective-permute-start.20 = (bf16[256,512]{1,0:T(8,128)(2,1)S(1)}, bf16[256,512]{1,0:T(8,128)(2,1)S(1)}, u32[]{:S(2)}, u32[]{:S(2)}) collective-permute-start(bf16[256,512]{1,0:T(8,128)(2,1)S(1)} %get-tuple-element.35), channel_id=1, source_target_pairs={{0,3},{1,2},{2,1},{3,0},{4,7},{5,6},{6,5},{7,4},{8,11},{9,10},{10,... | collective-permute-start | bytes 786440 | tf_op jit(solution)/shard_map/ppermute | solution.py:17
  172.5 15.7 %collective-permute-start = (bf16[256,512]{1,0:T(8,128)(2,1)}, bf16[256,512]{1,0:T(8,128)(2,1)}, u32[]{:S(2)}, u32[]{:S(2)}) collective-permute-start(bf16[256,512]{1,0:T(8,128)(2,1)} %get-tuple-element.33), channel_id=1, source_target_pairs={{0,1},{1,0},{2,3},{3,2},{4,5},{5,4},{6,7},{7,6},{8,9},{9,8},{10,11... | collective-permute-start | bytes 786440 | tf_op jit(solution)/shard_map/ppermute | solution.py:17
  172.6 16.2 %collective-permute-start.1 = (bf16[256,512]{1,0:T(8,128)(2,1)}, bf16[256,512]{1,0:T(8,128)(2,1)}, u32[]{:S(2)}, u32[]{:S(2)}) collective-permute-start(bf16[256,512]{1,0:T(8,128)(2,1)} %get-tuple-element.32), channel_id=1, source_target_pairs={{0,2},{1,3},{2,0},{3,1},{4,6},{5,7},{6,4},{7,5},{8,10},{9,11},{10,... | collective-permute-start | bytes 786440 | tf_op jit(solution)/shard_map/ppermute | solution.py:17
  173.8 20.8 %collective-permute-start.2 = (bf16[256,512]{1,0:T(8,128)(2,1)S(1)}, bf16[256,512]{1,0:T(8,128)(2,1)}, u32[]{:S(2)}, u32[]{:S(2)}) collective-permute-start(bf16[256,512]{1,0:T(8,128)(2,1)S(1)} %get-tuple-element.31), channel_id=1, source_target_pairs={{0,3},{1,2},{2,1},{3,0},{4,7},{5,6},{6,5},{7,4},{8,11},{9,10},{10,... | collective-permute-start | bytes 786440 | tf_op jit(solution)/shard_map/ppermute | solution.py:17
  243.1 33.0 %copy-start.9 = (bf16[1280,256]{0,1:T(8,128)(2,1)S(1)}, bf16[1280,256]{0,1:T(8,128)(2,1)}, u32[]{:S(2)}) copy-start(bf16[1280,256]{0,1:T(8,128)(2,1)} %copy-done.7) | copy-start | bytes 1966084
  281.2 10.5 %collective-permute-start.24 = (bf16[256,512]{0,1:T(8,128)(2,1)S(1)}, bf16[256,512]{0,1:T(8,128)(2,1)S(1)}, u32[]{:S(2)}, u32[]{:S(2)}) collective-permute-start(bf16[256,512]{0,1:T(8,128)(2,1)S(1)} %get-tuple-element.26), channel_id=1, source_target_pairs={{0,3},{1,2},{2,1},{3,0},{4,7},{5,6},{6,5},{7,4},{8,11},{9,10},{10,... | collective-permute-start | bytes 786440 | tf_op jit(solution)/shard_map/ppermute | solution.py:17
  284.6 12.8 %collective-permute-start.25 = (bf16[256,512]{0,1:T(8,128)(2,1)S(1)}, bf16[256,512]{0,1:T(8,128)(2,1)}, u32[]{:S(2)}, u32[]{:S(2)}) collective-permute-start(bf16[256,512]{0,1:T(8,128)(2,1)S(1)} %get-tuple-element.25), channel_id=1, source_target_pairs={{0,2},{1,3},{2,0},{3,1},{4,6},{5,7},{6,4},{7,5},{8,10},{9,11},{10,... | collective-permute-start | bytes 786440 | tf_op jit(solution)/shard_map/ppermute | solution.py:17
  284.9 12.6 %collective-permute-start.26 = (bf16[256,512]{0,1:T(8,128)(2,1)S(1)}, bf16[256,512]{0,1:T(8,128)(2,1)}, u32[]{:S(2)}, u32[]{:S(2)}) collective-permute-start(bf16[256,512]{0,1:T(8,128)(2,1)S(1)} %get-tuple-element.24), channel_id=1, source_target_pairs={{0,1},{1,0},{2,3},{3,2},{4,5},{5,4},{6,7},{7,6},{8,9},{9,8},{10,11... | collective-permute-start | bytes 786440 | tf_op jit(solution)/shard_map/ppermute | solution.py:17
  285.9 17.1 %collective-permute-start.21 = (bf16[256,512]{0,1:T(8,128)(2,1)}, bf16[256,512]{0,1:T(8,128)(2,1)}, u32[]{:S(2)}, u32[]{:S(2)}) collective-permute-start(bf16[256,512]{0,1:T(8,128)(2,1)} %get-tuple-element.29), channel_id=1, source_target_pairs={{0,3},{1,2},{2,1},{3,0},{4,7},{5,6},{6,5},{7,4},{8,11},{9,10},{10,... | collective-permute-start | bytes 786440 | tf_op jit(solution)/shard_map/ppermute | solution.py:17
  287.3 21.4 %collective-permute-start.22 = (bf16[256,512]{0,1:T(8,128)(2,1)}, bf16[256,512]{0,1:T(8,128)(2,1)}, u32[]{:S(2)}, u32[]{:S(2)}) collective-permute-start(bf16[256,512]{0,1:T(8,128)(2,1)} %get-tuple-element.28), channel_id=1, source_target_pairs={{0,2},{1,3},{2,0},{3,1},{4,6},{5,7},{6,4},{7,5},{8,10},{9,11},{10,... | collective-permute-start | bytes 786440 | tf_op jit(solution)/shard_map/ppermute | solution.py:17
  291.7 17.0 %collective-permute-start.23 = (bf16[256,512]{0,1:T(8,128)(2,1)S(1)}, bf16[256,512]{0,1:T(8,128)(2,1)}, u32[]{:S(2)}, u32[]{:S(2)}) collective-permute-start(bf16[256,512]{0,1:T(8,128)(2,1)S(1)} %get-tuple-element.27), channel_id=1, source_target_pairs={{0,1},{1,0},{2,3},{3,2},{4,5},{5,4},{6,7},{7,6},{8,9},{9,8},{10,11... | collective-permute-start | bytes 786440 | tf_op jit(solution)/shard_map/ppermute | solution.py:17
  (20 other events, 86.4 us)

commit v2 on v1

--- a/solution.py
+++ b/solution.py
@@ -1,6 +1,10 @@
+import functools
+
 import jax
 import jax.numpy as jnp
 from jax import lax
+from jax.experimental import pallas as pl
+from jax.experimental.pallas import tpu as pltpu
 from jax.sharding import PartitionSpec as P
 
 GROUP = 4
@@ -51,6 +55,162 @@
     return lax.all_to_all(
         block, "expert", split_axis=0, concat_axis=0, tiled=True, axis_index_groups=lists
     )
+
+
+CHUNKS = 2
+
+
+def rounds_kernel(
+    groups, block, hidden, hidden_t, picks, picks_t, weights, goal, master, first, second,
+    moved_out, first_out,
+    sum_out, sum_in, grad_out, grad_in, values, master_two, first_two, second_two, moved_one,
+    send_sems, recv_sems,
+):
+    bf16, f32 = jnp.bfloat16, jnp.float32
+    here = lax.axis_index("expert")
+    me, member = here // GROUP, lax.rem(here, GROUP)
+    units, width = master.shape
+    tokens = goal.shape[0]
+    top_count = picks.shape[0]
+    part = width // CHUNKS
+    unit_tile = units // GROUP
+    tok_tile = tokens // GROUP
+
+    barrier = pltpu.get_barrier_semaphore()
+    for d in range(1, groups):
+        peer = lax.rem(me + d, groups) * GROUP + member
+        pl.semaphore_signal(
+            barrier, inc=1, device_id={"expert": peer}, device_id_type=pl.DeviceIdType.MESH
+        )
+    pl.semaphore_wait(barrier, groups - 1)
+
+    def rows_of(group):
+        return pl.ds(pl.multiple_of(group * block, block), block)
+
+    def copy_to(source, target, phase, chunk, d):
+        ahead = lax.rem(me + d, groups)
+        return pltpu.make_async_remote_copy(
+            src_ref=source.at[phase // 2, chunk, rows_of(ahead)],
+            dst_ref=target.at[phase // 2, chunk, rows_of(me)],
+            send_sem=send_sems.at[phase, chunk, d - 1],
+            recv_sem=recv_sems.at[phase, chunk, d - 1],
+            device_id={"expert": ahead * GROUP + member},
+            device_id_type=pl.DeviceIdType.MESH,
+        )
+
+    order = list(range(1, groups)) + [0]
+
+    def spread(left, right, source, target, phase, chunk):
+        for d in order:
+            ahead = lax.rem(me + d, groups)
+            result = jnp.dot(
+                left[rows_of(ahead)], right, preferred_element_type=f32
+            ).astype(bf16)
+            if d:
+                source[phase // 2, chunk, rows_of(ahead)] = result
+                copy_to(source, target, phase, chunk, d).start()
+            else:
+                target[phase // 2, chunk, rows_of(ahead)] = result
+
+    def arrive(source, target, phase, chunk):
+        for d in range(1, groups):
+            copy_to(source, target, phase, chunk, d).wait_recv()
+
+    def columns(chunk):
+        return pl.ds(chunk * part, part)
+
+    def forward(step, chunk):
+        weight = master if step == 0 else master_two
+        spread(hidden, weight[:, columns(chunk)], sum_out, sum_in, 2 * step, chunk)
+
+    def residuals(step, chunk):
+        arrive(sum_out, sum_in, 2 * step, chunk)
+
+        @pl.loop(0, GROUP)
+        def _(tile):
+            span = pl.ds(pl.multiple_of(tile * tok_tile, tok_tile), tok_tile)
+            mixed = jnp.zeros((tok_tile, part), f32)
+            for k in range(top_count):
+                mixed = mixed + weights[k, span] * jnp.dot(
+                    picks[k, span], sum_in[step, chunk], preferred_element_type=f32
+                )
+            residual = (mixed - goal[span, columns(chunk)].astype(f32)) * loss_scale
+            for k in range(top_count):
+                place = pl.ds(
+                    pl.multiple_of(k * tokens + tile * tok_tile, tok_tile), tok_tile
+                )
+                values[place] = (weights[k, span] * residual).astype(bf16)
+
+        spread(picks_t, values[...], grad_out, grad_in, 2 * step + 1, chunk)
+
+    def update(step, chunk):
+        arrive(grad_out, grad_in, 2 * step + 1, chunk)
+        count = step + 1
+        first_fix = 1.0 - 0.9 ** (prior_steps + count)
+        second_fix = 1.0 - 0.999 ** (prior_steps + count)
+        cols = columns(chunk)
+
+        @pl.loop(0, GROUP)
+        def _(tile):
+            span = pl.ds(pl.multiple_of(tile * unit_tile, unit_tile), unit_tile)
+            gradient = jnp.dot(
+                hidden_t[span], grad_in[step, chunk], preferred_element_type=f32
+            )
+            one = (first if step == 0 else first_two)[span, cols].astype(f32)
+            two = (second if step == 0 else second_two)[span, cols].astype(f32)
+            one = 0.9 * one + 0.1 * gradient
+            two = 0.999 * two + 0.001 * gradient * gradient
+            change = (one / first_fix) / (jnp.sqrt(two / second_fix) + epsilon)
+            if step == 0:
+                first_two[span, cols] = one
+                second_two[span, cols] = two
+                moved_one[span, cols] = change
+                old = master[span, cols].astype(f32)
+                master_two[span, cols] = (old - learn_rate * change).astype(bf16)
+            else:
+                moved_out[span, cols] = (moved_one[span, cols] + change).astype(bf16)
+                first_out[span, cols] = one.astype(bf16)
+
+    for chunk in range(CHUNKS):
+        forward(0, chunk)
+    for step in range(2):
+        for chunk in range(CHUNKS):
+            residuals(step, chunk)
+        for chunk in range(CHUNKS):
+            update(step, chunk)
+            if step == 0:
+                forward(1, chunk)
+    for phase in range(4):
+        source, target = ((sum_out, sum_in), (grad_out, grad_in))[phase % 2]
+        for chunk in range(CHUNKS):
+            for d in range(1, groups):
+                copy_to(source, target, phase, chunk, d).wait_send()
+
+
+def refit(groups, block, hidden, hidden_t, picks, picks_t, weights, goal, master, first, second):
+    bf16, f32 = jnp.bfloat16, jnp.float32
+    units, width = master.shape
+    rows = hidden.shape[0]
+    travel = pltpu.VMEM((2, CHUNKS, rows, width // CHUNKS), bf16)
+    state = pltpu.VMEM((units, width), f32)
+    sems = pltpu.SemaphoreType.DMA((4, CHUNKS, groups - 1))
+    spec = pl.BlockSpec(memory_space=pltpu.VMEM)
+    return pl.pallas_call(
+        functools.partial(rounds_kernel, groups, block),
+        out_shape=[jax.ShapeDtypeStruct((units, width), bf16)] * 2,
+        in_specs=[spec] * 9,
+        out_specs=[spec] * 2,
+        scratch_shapes=[
+            travel, travel, travel, travel,
+            pltpu.VMEM((picks_t.shape[1], width // CHUNKS), bf16),
+            pltpu.VMEM((units, width), bf16),
+            state, state, state,
+            sems, sems,
+        ],
+        compiler_params=pltpu.CompilerParams(
+            collective_id=0, has_side_effects=True, vmem_limit_bytes=60 * 2**20
+        ),
+    )(hidden, hidden_t, picks, picks_t, weights, goal, master, first, second)
 
 
 def shards(tokens, targets, routes, gate_ints, expert_home, gate_up, down_master, moment1, moment2):
@@ -83,11 +243,19 @@
         jnp.stack([slot_dest.T, gate_ints.T], axis=1)[None], 0
     )
     all_dest, all_gates = plan[:, :, 0], plan[:, :, 1]
-    weights = all_gates.astype(f32) / 4096.0
-    picks = (all_dest[:, :, :, None] == row_ids).astype(bf16)
+    block = -(-GROUP * capacity // 16) * 16
+    rows = groups * block
+    offsets = (jnp.arange(GROUP, dtype=jnp.int32) * capacity)[:, None, None]
+    all_dest = all_dest // capacity * block + all_dest % capacity + offsets
+    by_choice = all_dest.transpose(1, 0, 2).reshape(top_count, GROUP * tok_rows)
+    weights = all_gates.transpose(1, 0, 2).reshape(top_count, GROUP * tok_rows, 1)
+    weights = weights.astype(f32) / 4096.0
+    buffer_ids = jnp.arange(rows, dtype=jnp.int32)
+    picks = (by_choice[:, :, None] == buffer_ids).astype(bf16)
+    picks_t = (buffer_ids[:, None] == by_choice.reshape(-1)).astype(bf16)
 
     arrived = member_gather(over_groups(outgoing), 1)
-    rows = groups * GROUP * capacity
+    arrived = jnp.pad(arrived, ((0, 0), (0, block - GROUP * capacity), (0, 0)))
     arrived = arrived.reshape(rows, feat_width)
 
     master = to_slices(down_master.astype(bf16), member)
@@ -96,10 +264,10 @@
     moment_two = to_slices(moment2.astype(bf16), member)
     units = master.shape[1]
     flat = (GROUP * units, width)
-    master = master.reshape(flat).astype(f32)
-    moment_one = moment_one.reshape(flat).astype(f32)
-    moment_two = moment_two.reshape(flat).astype(f32)
-    goal = goal.astype(f32)
+    master = master.reshape(flat)
+    moment_one = moment_one.reshape(flat)
+    moment_two = moment_two.reshape(flat)
+    goal = goal.reshape(GROUP * tok_rows, width)
 
     gate_acts = lax.dot_general(
         arrived, gate_up[0], (((1,), (1,)), ((), ())), preferred_element_type=f32
@@ -107,56 +275,33 @@
     up_acts = lax.dot_general(
         arrived, gate_up[1], (((1,), (1,)), ((), ())), preferred_element_type=f32
     )
+    def reordered(piece, mask):
+        piece = piece.reshape(groups, block, -1)
+        parts = [
+            piece[:, (i ^ mask) * capacity : ((i ^ mask) + 1) * capacity] for i in range(GROUP)
+        ]
+        parts.append(piece[:, GROUP * capacity :])
+        return jnp.concatenate(parts, axis=1).reshape(rows, -1)
+
     own_hidden = (jax.nn.silu(gate_acts) * up_acts).astype(bf16)
     across = flipped(own_hidden, 2)
     hiddens = [own_hidden, flipped(own_hidden, 1), across, flipped(across, 1)]
     hidden = jnp.concatenate(
         [
-            jnp.stack(
-                [block.reshape(groups, GROUP, capacity, -1)[:, i ^ mask] for i in range(GROUP)],
-                axis=1,
-            ).reshape(rows, -1)
-            for mask, block in enumerate(hiddens)
+            reordered(piece, mask)
+            for mask, piece in enumerate(hiddens)
         ],
         axis=1,
     )
 
-    moved = jnp.zeros(flat, f32)
-    for round_index in range(2):
-        summed = jnp.dot(hidden, master.astype(bf16), preferred_element_type=f32).astype(bf16)
-        returned = over_groups(summed.reshape(groups, GROUP, capacity, width))
-        returned = returned.transpose(1, 0, 2, 3).reshape(GROUP, slot_rows, width)
-        mixed = jnp.zeros((GROUP, tok_rows, width), f32)
-        for k in range(top_count):
-            picked = jnp.einsum(
-                "mts,msc->mtc", picks[:, k], returned, preferred_element_type=f32
-            )
-            mixed = mixed + weights[:, k, :, None] * picked
-        residual = (mixed - goal) * loss_scale
-        slot_values = (weights[:, :, :, None] * residual[:, None]).astype(bf16)
-        grads_out = jnp.einsum(
-            "mks,mkc->msc",
-            picks.reshape(GROUP, top_count * tok_rows, slot_rows),
-            slot_values.reshape(GROUP, top_count * tok_rows, width),
-            preferred_element_type=f32,
-        ).astype(bf16)
-        grads_out = grads_out.reshape(GROUP, groups, capacity, width).transpose(1, 0, 2, 3)
-        grad_rows = over_groups(grads_out).reshape(rows, width)
-        gradient = lax.dot_general(
-            hidden, grad_rows, (((0,), (0,)), ((), ())), preferred_element_type=f32
-        )
-        count = round_index + 1
-        moment_one = 0.9 * moment_one + 0.1 * gradient
-        moment_two = 0.999 * moment_two + 0.001 * gradient * gradient
-        first_fix = 1.0 - 0.9 ** (prior_steps + count)
-        second_fix = 1.0 - 0.999 ** (prior_steps + count)
-        change = (moment_one / first_fix) / (jnp.sqrt(moment_two / second_fix) + epsilon)
-        moved = moved + change
-        master = master - learn_rate * change
+    moved, moment_one = refit(
+        groups, block, hidden, hidden.T, picks, picks_t, weights, goal,
+        master, moment_one, moment_two,
+    )
     shape = (GROUP, units, width)
     return (
-        to_rows(moved.astype(bf16).reshape(shape), member).astype(f32),
-        to_rows(moment_one.astype(bf16).reshape(shape), member).astype(f32),
+        to_rows(moved.reshape(shape), member).astype(f32),
+        to_rows(moment_one.reshape(shape), member).astype(f32),
     )
 
 

time: 315 us -> 298 us (0.946)
  Pallas kernels: 0 us -> 126 us
  blocking collectives: 100 us -> 33.2 us
  waiting for transfers between devices: 106 us -> 66.3 us
  matrix products: 26.8 us -> 3.76 us
  starting transfers between devices: 40.8 us -> 24.3 us
  other arithmetic: 16.6 us -> 28.6 us
  local copies, waits for them, and re-layouts: 20.9 us -> 14.1 us
    pallas_call x0 -> x1, Pallas kernels: none -> 126 us  [refit(): pl.pallas_call(functools.partial(rounds_kernel, groups, block), out_shape...]
    all_to_all x3 -> x1, blocking collectives: 100 us -> 33.2 us  [over_groups(): lax.all_to_all(block, 'expert', split_axis=0, concat_axis=0, tiled=True,...]
    dot_general x10 -> x0, matrix products: 22.2 us -> none  [the longest x2 9.61 us: shards(): lax.dot_general(hidden, grad_rows, (((0,), (0,)), ((), ())), preferred_el...]
    all_to_all x2 -> x0, waiting for transfers between devices: 21.1 us -> none  [over_groups(): lax.all_to_all(block, 'expert', split_axis=0, concat_axis=0, tiled=True,...]
    ppermute x27, waiting for transfers between devices: 84.4 us -> 66.3 us  [flipped(): return lax.ppermute(block, 'expert', [(i, i ^ mask) for i in range(count)])]
    all_to_all x2 -> x0, starting transfers between devices: 12.8 us -> none  [over_groups(): lax.all_to_all(block, 'expert', split_axis=0, concat_axis=0, tiled=True,...]
    convert_element_type x4, other arithmetic: 0.72 us -> 7.81 us  [the longest x1 2.71 us: shards(): picks_t = (buffer_ids[:, None] == by_choice.reshape(-1)).astype(bf16)]
    another operation x1 -> x4, other arithmetic: 0.13 us -> 7.21 us  [to_slices(): return jnp.stack(pieces)]
  transfers between devices with their start and end apart: 29 -> 27, of which waited for: 14 -> 10; matrix products, arithmetic and copies ran while one was open for 7% -> 11% of each run, Pallas kernels for 0% -> 0%
where the time goes in v2:
time: 298 us; the launch traced here: 297 us
  Pallas kernels  126 us (42%)
  waiting for transfers between devices  66.3 us (22%)
  blocking collectives  33.2 us (11%)
  other arithmetic  28.6 us (10%)
  starting transfers between devices  24.3 us (8%)
  local copies, waits for them, and re-layouts  14.1 us (5%)
  matrix products  3.76 us (1%)
    pallas_call x1, Pallas kernels, refit(): pl.pallas_call(functools.partial(rounds_kernel, groups, block), out_shape...  126 us
    ppermute x27, waiting for transfers between devices, flipped(): return lax.ppermute(block, 'expert', [(i, i ^ mask) for i in range(count)])  66.3 us
    all_to_all x1, blocking collectives, over_groups(): lax.all_to_all(block, 'expert', split_axis=0, concat_axis=0, tiled=True,...  33.2 us
    ppermute x27, starting transfers between devices, flipped(): return lax.ppermute(block, 'expert', [(i, i ^ mask) for i in range(count)])  24.3 us
    another operation x4, other arithmetic, to_slices(): return jnp.stack(pieces)  7.21 us
  transfers between devices with their start and end apart: 27, of which 10 were waited for; matrix products, arithmetic and copies ran while one was open for 11% of the time, Pallas kernels for 0%

profile of v2, /device:TPU:11, one launch (start us, length us, event | category | flops | bytes accessed | tf_op | source)
XLA Modules:
  0.0 297.2 jit_solution(16108012204954903793)
XLA Ops:
  5.0 33.2 %all_to_all.5 = bf16[4,80,2048]{2,1,0:T(8,128)(2,1)S(1)} all-to-all(bf16[4,80,2048]{2,1,0:T(8,128)(2,1)S(1)} %bitcast.147), channel_id=1, replica_groups={{0,4,8,12},{1,5,9,13},{2,6,10,14},{3,7,11,15},{16,20,24,28},{17,21,25,2..., dimensions={0} | all-to-all | bytes 2621440 | tf_op jit(solution)/shard_map/all_to_all | solution.py:55
  39.8 2.7 collective-permute-start.6
  42.5 1.7 convert_element_type.56
  44.5 1.3 collective-permute-start.13
  48.6 18.0 %collective-permute-done.7 = s32[1,2,2,128]{3,2,1,0:T(2,128)S(1)} collective-permute-done((s32[1,2,2,128]{3,2,1,0:T(2,128)S(1)}, s32[1,2,2,128]{3,2,1,0:T(2,128)S(1)}, u32[]{:S(2)}, u32[]{:S(2)}) %collective-permute-start.7) | collective-permute-done | bytes 2080 | tf_op jit(solution)/shard_map/ppermute | solution.py:21
  66.6 5.5 %collective-permute-start.8 = (s32[1,2,2,128]{3,2,1,0:T(2,128)S(1)}, s32[1,2,2,128]{3,2,1,0:T(2,128)S(1)}, u32[]{:S(2)}, u32[]{:S(2)}) collective-permute-start(s32[1,2,2,128]{3,2,1,0:T(2,128)S(1)} %collective-permute-done.7), channel_id=1, source_target_pairs={{0,1},{1,0},{2,3},{3,2},{4,5},{5,4},{6,7},{7,6},{8,9},{9,8},{10,11... | collective-permute-start | bytes 6152 | tf_op jit(solution)/shard_map/ppermute | solution.py:21
  74.0 2.0 fusion.picks
  76.0 2.7 fusion.1.picks_t
  79.9 5.1 %pad_maximum_fusion = bf16[4,320,2048]{2,1,0:T(8,128)(2,1)S(1)} fusion(bf16[4,80,2048]{2,1,0:T(8,128)(2,1)S(1)} %collective-permute-done.2, bf16[4,80,2048]{2,1,0:T(8,128)(2,1)} %collective-permute-done.1, bf16[4,80,2048]{2,1,0:T(8,128)(2,1)S(1)} %collective-permute-done, bf16[4,80,2048]{2,1,0:T(8,128)(2,1)S(1)} %all_to_all.5), kind=kLoop, calls=%fused_computation | loop fusion | flops 20971520 | bytes 10485760 | tf_op jit(solution)/shard_map/concatenate | solution.py:28
  85.0 1.6 fusion.6
  87.7 1.7 multiply_convert_fusion
  89.6 2.7 collective-permute-done.11
  92.9 1.4 collective-permute-start.17
  96.3 1.8 pad_maximum_fusion.8
  98.7 1.4 collective-permute-done.16
  100.7 6.4 %collective-permute-done.17 = bf16[256,512]{1,0:T(8,128)(2,1)} collective-permute-done((bf16[256,512]{1,0:T(8,128)(2,1)}, bf16[256,512]{1,0:T(8,128)(2,1)}, u32[]{:S(2)}, u32[]{:S(2)}) %collective-permute-start.17) | collective-permute-done | bytes 262176 | tf_op jit(solution)/shard_map/ppermute | solution.py:21
  107.1 2.2 pad_maximum_fusion.2
  109.3 2.1 pad_maximum_fusion.3
  111.5 13.8 %collective-permute-done.19 = bf16[256,512]{1,0:T(8,128)(2,1)S(1)} collective-permute-done((bf16[256,512]{1,0:T(8,128)(2,1)S(1)}, bf16[256,512]{1,0:T(8,128)(2,1)S(1)}, u32[]{:S(2)}, u32[]{:S(2)}) %collective-permute-start.19) | collective-permute-done | bytes 262176 | tf_op jit(solution)/shard_map/ppermute | solution.py:21
  125.3 6.2 %collective-permute-done.20 = bf16[256,512]{1,0:T(8,128)(2,1)S(1)} collective-permute-done((bf16[256,512]{1,0:T(8,128)(2,1)S(1)}, bf16[256,512]{1,0:T(8,128)(2,1)S(1)}, u32[]{:S(2)}, u32[]{:S(2)}) %collective-permute-start.20) | collective-permute-done | bytes 262176 | tf_op jit(solution)/shard_map/ppermute | solution.py:21
  133.2 1.3 copy.61
  137.2 2.9 fusion.27
  140.1 2.7 copy.74.hidden
  142.8 125.9 %shard_map.104 = (bf16[1024,512]{1,0:T(8,128)(2,1)}, bf16[1024,512]{1,0:T(8,128)(2,1)}) custom-call(bf16[1280,1024]{1,0:T(8,128)(2,1)} %copy.74.hidden, bf16[1024,1280]{1,0:T(8,128)(2,1)} %get-tuple-element.10.hidden_t, bf16[2,512,1280]{2,1,0:T(8,128)(2,1)} %fusion.picks, bf16[1280,1024]{1,0:T(8,128)(2,1)} %fusion.1.picks_t, f32[2,512,1]{2,1,0:T(8,128)} %div.33.weights, ...), custom_call_target="tpu_custom_call" | custom-call | tf_op jit(solution)/shard_map/pallas_call | solution.py:198
  268.7 1.2 fusion.28
  269.9 1.5 collective-permute-start.24
  274.3 4.4 %collective-permute-done.24 = bf16[256,512]{1,0:T(8,128)(2,1)S(1)} collective-permute-done((bf16[256,512]{1,0:T(8,128)(2,1)S(1)}, bf16[256,512]{1,0:T(8,128)(2,1)S(1)}, u32[]{:S(2)}, u32[]{:S(2)}) %collective-permute-start.24) | collective-permute-done | bytes 262176 | tf_op jit(solution)/shard_map/ppermute | solution.py:21
  279.5 4.9 %collective-permute-done.25 = bf16[256,512]{1,0:T(8,128)(2,1)S(1)} collective-permute-done((bf16[256,512]{1,0:T(8,128)(2,1)S(1)}, bf16[256,512]{1,0:T(8,128)(2,1)S(1)}, u32[]{:S(2)}, u32[]{:S(2)}) %collective-permute-start.25) | collective-permute-done | bytes 262176 | tf_op jit(solution)/shard_map/ppermute | solution.py:21
  285.5 1.6 maximum_convert_fusion.1
  287.1 2.8 collective-permute-done.21
  289.9 5.6 %collective-permute-done.22 = bf16[256,512]{1,0:T(8,128)(2,1)S(1)} collective-permute-done((bf16[256,512]{1,0:T(8,128)(2,1)S(1)}, bf16[256,512]{1,0:T(8,128)(2,1)S(1)}, u32[]{:S(2)}, u32[]{:S(2)}) %collective-permute-start.22) | collective-permute-done | bytes 262176 | tf_op jit(solution)/shard_map/ppermute | solution.py:21
  295.6 1.6 maximum_convert_fusion
  (117 shorter events, 26.2 us)
Async XLA Ops:
  4.5 35.0 %copy-start.14 = (s32[128,2]{0,1:T(2,128)S(1)}, s32[128,2]{0,1:T(2,128)}, u32[]{:S(2)}) copy-start(s32[128,2]{0,1:T(2,128)} %param.12) | copy-start | bytes 3076
  38.2 35.6 %collective-permute-start.1 = (bf16[4,80,2048]{2,1,0:T(8,128)(2,1)S(1)}, bf16[4,80,2048]{2,1,0:T(8,128)(2,1)}, u32[]{:S(2)}, u32[]{:S(2)}) collective-permute-start(bf16[4,80,2048]{2,1,0:T(8,128)(2,1)S(1)} %all_to_all.5), channel_id=1, source_target_pairs={{0,2},{1,3},{2,0},{3,1},{4,6},{5,7},{6,4},{7,5},{8,10},{9,11},{10,... | collective-permute-start | bytes 3932168 | tf_op jit(solution)/shard_map/ppermute | solution.py:21
  39.6 27.0 %collective-permute-start.7 = (s32[1,2,2,128]{3,2,1,0:T(2,128)S(1)}, s32[1,2,2,128]{3,2,1,0:T(2,128)S(1)}, u32[]{:S(2)}, u32[]{:S(2)}) collective-permute-start(s32[1,2,2,128]{3,2,1,0:T(2,128)S(1)} %get-tuple-element.53), channel_id=1, source_target_pairs={{0,2},{1,3},{2,0},{3,1},{4,6},{5,7},{6,4},{7,5},{8,10},{9,11},{10,... | collective-permute-start | bytes 6152 | tf_op jit(solution)/shard_map/ppermute | solution.py:21
  39.8 32.2 %collective-permute-start.6 = (s32[1,2,2,128]{3,2,1,0:T(2,128)S(1)}, s32[1,2,2,128]{3,2,1,0:T(2,128)S(1)}, u32[]{:S(2)}, u32[]{:S(2)}) collective-permute-start(s32[1,2,2,128]{3,2,1,0:T(2,128)S(1)} %get-tuple-element.53), channel_id=1, source_target_pairs={{0,1},{1,0},{2,3},{3,2},{4,5},{5,4},{6,7},{7,6},{8,9},{9,8},{10,11... | collective-permute-start | bytes 6152 | tf_op jit(solution)/shard_map/ppermute | solution.py:21
  44.4 48.5 %collective-permute-start.12 = (bf16[256,512]{1,0:T(8,128)(2,1)S(1)}, bf16[256,512]{1,0:T(8,128)(2,1)S(1)}, u32[]{:S(2)}, u32[]{:S(2)}) collective-permute-start(bf16[256,512]{1,0:T(8,128)(2,1)S(1)} %get-tuple-element.37), channel_id=1, source_target_pairs={{0,1},{1,0},{2,3},{3,2},{4,5},{5,4},{6,7},{7,6},{8,9},{9,8},{10,11... | collective-permute-start | bytes 786440 | tf_op jit(solution)/shard_map/ppermute | solution.py:21
  44.5 49.8 %collective-permute-start.13 = (bf16[256,512]{1,0:T(8,128)(2,1)S(1)}, bf16[256,512]{1,0:T(8,128)(2,1)S(1)}, u32[]{:S(2)}, u32[]{:S(2)}) collective-permute-start(bf16[256,512]{1,0:T(8,128)(2,1)S(1)} %get-tuple-element.36), channel_id=1, source_target_pairs={{0,2},{1,3},{2,0},{3,1},{4,6},{5,7},{6,4},{7,5},{8,10},{9,11},{10,... | collective-permute-start | bytes 786440 | tf_op jit(solution)/shard_map/ppermute | solution.py:21
  66.6 6.7 %collective-permute-start.8 = (s32[1,2,2,128]{3,2,1,0:T(2,128)S(1)}, s32[1,2,2,128]{3,2,1,0:T(2,128)S(1)}, u32[]{:S(2)}, u32[]{:S(2)}) collective-permute-start(s32[1,2,2,128]{3,2,1,0:T(2,128)S(1)} %collective-permute-done.7), channel_id=1, source_target_pairs={{0,1},{1,0},{2,3},{3,2},{4,5},{5,4},{6,7},{7,6},{8,9},{9,8},{10,11... | collective-permute-start | bytes 6152 | tf_op jit(solution)/shard_map/ppermute | solution.py:21
  72.1 22.3 %collective-permute-start.14 = (bf16[256,512]{1,0:T(8,128)(2,1)S(1)}, bf16[256,512]{1,0:T(8,128)(2,1)S(1)}, u32[]{:S(2)}, u32[]{:S(2)}) collective-permute-start(bf16[256,512]{1,0:T(8,128)(2,1)S(1)} %get-tuple-element.35), channel_id=1, source_target_pairs={{0,3},{1,2},{2,1},{3,0},{4,7},{5,6},{6,5},{7,4},{8,11},{9,10},{10,... | collective-permute-start | bytes 786440 | tf_op jit(solution)/shard_map/ppermute | solution.py:21
  73.4 5.3 %collective-permute-start = (bf16[4,80,2048]{2,1,0:T(8,128)(2,1)S(1)}, bf16[4,80,2048]{2,1,0:T(8,128)(2,1)S(1)}, u32[]{:S(2)}, u32[]{:S(2)}) collective-permute-start(bf16[4,80,2048]{2,1,0:T(8,128)(2,1)S(1)} %all_to_all.5), channel_id=1, source_target_pairs={{0,1},{1,0},{2,3},{3,2},{4,5},{5,4},{6,7},{7,6},{8,9},{9,8},{10,11... | collective-permute-start | bytes 3932168 | tf_op jit(solution)/shard_map/ppermute | solution.py:21
  73.8 5.3 %collective-permute-start.2 = (bf16[4,80,2048]{2,1,0:T(8,128)(2,1)}, bf16[4,80,2048]{2,1,0:T(8,128)(2,1)S(1)}, u32[]{:S(2)}, u32[]{:S(2)}) collective-permute-start(bf16[4,80,2048]{2,1,0:T(8,128)(2,1)} %collective-permute-done.1), channel_id=1, source_target_pairs={{0,1},{1,0},{2,3},{3,2},{4,5},{5,4},{6,7},{7,6},{8,9},{9,8},{10,11... | collective-permute-start | bytes 3932168 | tf_op jit(solution)/shard_map/ppermute | solution.py:21
  78.7 7.9 %collective-permute-start.9 = (bf16[128,512]{1,0:T(8,128)(2,1)S(1)}, bf16[128,512]{1,0:T(8,128)(2,1)S(1)}, u32[]{:S(2)}, u32[]{:S(2)}) collective-permute-start(bf16[128,512]{1,0:T(8,128)(2,1)S(1)} %get-tuple-element.49), channel_id=1, source_target_pairs={{0,1},{1,0},{2,3},{3,2},{4,5},{5,4},{6,7},{7,6},{8,9},{9,8},{10,11... | collective-permute-start | bytes 393224 | tf_op jit(solution)/shard_map/ppermute | solution.py:21
  79.1 10.3 %collective-permute-start.10 = (bf16[128,512]{1,0:T(8,128)(2,1)S(1)}, bf16[128,512]{1,0:T(8,128)(2,1)S(1)}, u32[]{:S(2)}, u32[]{:S(2)}) collective-permute-start(bf16[128,512]{1,0:T(8,128)(2,1)S(1)} %get-tuple-element.51), channel_id=1, source_target_pairs={{0,2},{1,3},{2,0},{3,1},{4,6},{5,7},{6,4},{7,5},{8,10},{9,11},{10,... | collective-permute-start | bytes 393224 | tf_op jit(solution)/shard_map/ppermute | solution.py:21
  86.6 11.4 %copy-start.9 = (bf16[256,512]{1,0:T(8,128)(2,1)S(1)}, bf16[256,512]{1,0:T(8,128)(2,1)}, u32[]{:S(2)}) copy-start(bf16[256,512]{1,0:T(8,128)(2,1)} %get-tuple-element.29) | copy-start | bytes 786436
  86.6 13.5 %copy-start.8 = (bf16[256,512]{1,0:T(8,128)(2,1)S(1)}, bf16[256,512]{1,0:T(8,128)(2,1)}, u32[]{:S(2)}) copy-start(bf16[256,512]{1,0:T(8,128)(2,1)} %get-tuple-element.28) | copy-start | bytes 786436
  86.6 20.5 %copy-start.7 = (bf16[256,512]{1,0:T(8,128)(2,1)S(1)}, bf16[256,512]{1,0:T(8,128)(2,1)}, u32[]{:S(2)}) copy-start(bf16[256,512]{1,0:T(8,128)(2,1)} %get-tuple-element.27) | copy-start | bytes 786436
  86.6 5.7 %collective-permute-start.11 = (bf16[128,512]{1,0:T(8,128)(2,1)S(1)}, bf16[128,512]{1,0:T(8,128)(2,1)S(1)}, u32[]{:S(2)}, u32[]{:S(2)}) collective-permute-start(bf16[128,512]{1,0:T(8,128)(2,1)S(1)} %get-tuple-element.50), channel_id=1, source_target_pairs={{0,3},{1,2},{2,1},{3,0},{4,7},{5,6},{6,5},{7,4},{8,11},{9,10},{10,... | collective-permute-start | bytes 393224 | tf_op jit(solution)/shard_map/ppermute | solution.py:21
  89.4 43.6 %copy-start.5 = (bf16[1280,256]{0,1:T(8,128)(2,1)}, bf16[1280,256]{0,1:T(8,128)(2,1)S(1)}, u32[]{:S(2)}) copy-start(bf16[1280,256]{0,1:T(8,128)(2,1)S(1)} %multiply_convert_fusion) | copy-start | bytes 1966084
  89.4 8.6 %collective-permute-start.15 = (bf16[256,512]{1,0:T(8,128)(2,1)}, bf16[256,512]{1,0:T(8,128)(2,1)S(1)}, u32[]{:S(2)}, u32[]{:S(2)}) collective-permute-start(bf16[256,512]{1,0:T(8,128)(2,1)} %get-tuple-element.33), channel_id=1, source_target_pairs={{0,1},{1,0},{2,3},{3,2},{4,5},{5,4},{6,7},{7,6},{8,9},{9,8},{10,11... | collective-permute-start | bytes 786440 | tf_op jit(solution)/shard_map/ppermute | solution.py:21
  92.3 7.8 %collective-permute-start.16 = (bf16[256,512]{1,0:T(8,128)(2,1)}, bf16[256,512]{1,0:T(8,128)(2,1)}, u32[]{:S(2)}, u32[]{:S(2)}) collective-permute-start(bf16[256,512]{1,0:T(8,128)(2,1)} %get-tuple-element.32), channel_id=1, source_target_pairs={{0,2},{1,3},{2,0},{3,1},{4,6},{5,7},{6,4},{7,5},{8,10},{9,11},{10,... | collective-permute-start | bytes 786440 | tf_op jit(solution)/shard_map/ppermute | solution.py:21
  92.9 14.2 %collective-permute-start.17 = (bf16[256,512]{1,0:T(8,128)(2,1)}, bf16[256,512]{1,0:T(8,128)(2,1)}, u32[]{:S(2)}, u32[]{:S(2)}) collective-permute-start(bf16[256,512]{1,0:T(8,128)(2,1)} %get-tuple-element.31), channel_id=1, source_target_pairs={{0,3},{1,2},{2,1},{3,0},{4,7},{5,6},{6,5},{7,4},{8,11},{9,10},{10,... | collective-permute-start | bytes 786440 | tf_op jit(solution)/shard_map/ppermute | solution.py:21
  94.3 38.2 %collective-permute-start.3 = (bf16[1280,256]{0,1:T(8,128)(2,1)S(1)}, bf16[1280,256]{0,1:T(8,128)(2,1)S(1)}, u32[]{:S(2)}, u32[]{:S(2)}) collective-permute-start(bf16[1280,256]{0,1:T(8,128)(2,1)S(1)} %multiply_convert_fusion), channel_id=1, source_target_pairs={{0,1},{1,0},{2,3},{3,2},{4,5},{5,4},{6,7},{7,6},{8,9},{9,8},{10,11... | collective-permute-start | bytes 1966088 | tf_op jit(solution)/shard_map/ppermute | solution.py:21
  94.4 38.4 %collective-permute-start.4 = (bf16[1280,256]{0,1:T(8,128)(2,1)S(1)}, bf16[1280,256]{0,1:T(8,128)(2,1)}, u32[]{:S(2)}, u32[]{:S(2)}) collective-permute-start(bf16[1280,256]{0,1:T(8,128)(2,1)S(1)} %multiply_convert_fusion), channel_id=1, source_target_pairs={{0,2},{1,3},{2,0},{3,1},{4,6},{5,7},{6,4},{7,5},{8,10},{9,11},{10,... | collective-permute-start | bytes 1966088 | tf_op jit(solution)/shard_map/ppermute | solution.py:21
  98.0 13.4 %collective-permute-start.18 = (bf16[256,512]{1,0:T(8,128)(2,1)S(1)}, bf16[256,512]{1,0:T(8,128)(2,1)S(1)}, u32[]{:S(2)}, u32[]{:S(2)}) collective-permute-start(bf16[256,512]{1,0:T(8,128)(2,1)S(1)} %copy-done.9), channel_id=1, source_target_pairs={{0,1},{1,0},{2,3},{3,2},{4,5},{5,4},{6,7},{7,6},{8,9},{9,8},{10,11... | collective-permute-start | bytes 786440 | tf_op jit(solution)/shard_map/ppermute | solution.py:21
  100.1 25.2 %collective-permute-start.19 = (bf16[256,512]{1,0:T(8,128)(2,1)S(1)}, bf16[256,512]{1,0:T(8,128)(2,1)S(1)}, u32[]{:S(2)}, u32[]{:S(2)}) collective-permute-start(bf16[256,512]{1,0:T(8,128)(2,1)S(1)} %copy-done.8), channel_id=1, source_target_pairs={{0,2},{1,3},{2,0},{3,1},{4,6},{5,7},{6,4},{7,5},{8,10},{9,11},{10,... | collective-permute-start | bytes 786440 | tf_op jit(solution)/shard_map/ppermute | solution.py:21
  107.1 24.3 %collective-permute-start.20 = (bf16[256,512]{1,0:T(8,128)(2,1)S(1)}, bf16[256,512]{1,0:T(8,128)(2,1)S(1)}, u32[]{:S(2)}, u32[]{:S(2)}) collective-permute-start(bf16[256,512]{1,0:T(8,128)(2,1)S(1)} %copy-done.7), channel_id=1, source_target_pairs={{0,3},{1,2},{2,1},{3,0},{4,7},{5,6},{6,5},{7,4},{8,11},{9,10},{10,... | collective-permute-start | bytes 786440 | tf_op jit(solution)/shard_map/ppermute | solution.py:21
  132.8 2.9 collective-permute-start.5
  269.9 8.7 %collective-permute-start.24 = (bf16[256,512]{1,0:T(8,128)(2,1)S(1)}, bf16[256,512]{1,0:T(8,128)(2,1)S(1)}, u32[]{:S(2)}, u32[]{:S(2)}) collective-permute-start(bf16[256,512]{1,0:T(8,128)(2,1)S(1)} %get-tuple-element.22), channel_id=1, source_target_pairs={{0,3},{1,2},{2,1},{3,0},{4,7},{5,6},{6,5},{7,4},{8,11},{9,10},{10,... | collective-permute-start | bytes 786440 | tf_op jit(solution)/shard_map/ppermute | solution.py:21
  271.4 13.1 %collective-permute-start.25 = (bf16[256,512]{1,0:T(8,128)(2,1)S(1)}, bf16[256,512]{1,0:T(8,128)(2,1)S(1)}, u32[]{:S(2)}, u32[]{:S(2)}) collective-permute-start(bf16[256,512]{1,0:T(8,128)(2,1)S(1)} %get-tuple-element.21), channel_id=1, source_target_pairs={{0,2},{1,3},{2,0},{3,1},{4,6},{5,7},{6,4},{7,5},{8,10},{9,11},{10,... | collective-permute-start | bytes 786440 | tf_op jit(solution)/shard_map/ppermute | solution.py:21
  272.3 12.2 %collective-permute-start.26 = (bf16[256,512]{1,0:T(8,128)(2,1)S(1)}, bf16[256,512]{1,0:T(8,128)(2,1)S(1)}, u32[]{:S(2)}, u32[]{:S(2)}) collective-permute-start(bf16[256,512]{1,0:T(8,128)(2,1)S(1)} %get-tuple-element.20), channel_id=1, source_target_pairs={{0,1},{1,0},{2,3},{3,2},{4,5},{5,4},{6,7},{7,6},{8,9},{9,8},{10,11... | collective-permute-start | bytes 786440 | tf_op jit(solution)/shard_map/ppermute | solution.py:21
  272.3 17.6 %collective-permute-start.21 = (bf16[256,512]{1,0:T(8,128)(2,1)S(1)}, bf16[256,512]{1,0:T(8,128)(2,1)S(1)}, u32[]{:S(2)}, u32[]{:S(2)}) collective-permute-start(bf16[256,512]{1,0:T(8,128)(2,1)S(1)} %get-tuple-element.25), channel_id=1, source_target_pairs={{0,3},{1,2},{2,1},{3,0},{4,7},{5,6},{6,5},{7,4},{8,11},{9,10},{10,... | collective-permute-start | bytes 786440 | tf_op jit(solution)/shard_map/ppermute | solution.py:21
  273.4 22.1 %collective-permute-start.22 = (bf16[256,512]{1,0:T(8,128)(2,1)S(1)}, bf16[256,512]{1,0:T(8,128)(2,1)S(1)}, u32[]{:S(2)}, u32[]{:S(2)}) collective-permute-start(bf16[256,512]{1,0:T(8,128)(2,1)S(1)} %get-tuple-element.24), channel_id=1, source_target_pairs={{0,2},{1,3},{2,0},{3,1},{4,6},{5,7},{6,4},{7,5},{8,10},{9,11},{10,... | collective-permute-start | bytes 786440 | tf_op jit(solution)/shard_map/ppermute | solution.py:21
  278.7 16.9 %collective-permute-start.23 = (bf16[256,512]{1,0:T(8,128)(2,1)S(1)}, bf16[256,512]{1,0:T(8,128)(2,1)S(1)}, u32[]{:S(2)}, u32[]{:S(2)}) collective-permute-start(bf16[256,512]{1,0:T(8,128)(2,1)S(1)} %get-tuple-element.23), channel_id=1, source_target_pairs={{0,1},{1,0},{2,3},{3,2},{4,5},{5,4},{6,7},{7,6},{8,9},{9,8},{10,11... | collective-permute-start | bytes 786440 | tf_op jit(solution)/shard_map/ppermute | solution.py:21
  (11 other events, 29.2 us)

commit v3 on v2

--- a/solution.py
+++ b/solution.py
@@ -21,23 +21,203 @@
     return lax.ppermute(block, "expert", [(i, i ^ mask) for i in range(count)])
 
 
+def partner_of(member, mask):
+    low, high = lax.rem(member, 2), member // 2
+    return member + (mask & 1) * (1 - 2 * low) + (mask & 2) * (1 - 2 * high)
+
+
+def greet(peers):
+    barrier = pltpu.get_barrier_semaphore()
+    for peer in peers:
+        pl.semaphore_signal(
+            barrier, inc=1, device_id={"expert": peer}, device_id_type=pl.DeviceIdType.MESH
+        )
+    pl.semaphore_wait(barrier, len(peers))
+
+
+def push(source, target, send_sem, recv_sem, peer):
+    return pltpu.make_async_remote_copy(
+        src_ref=source,
+        dst_ref=target,
+        send_sem=send_sem,
+        recv_sem=recv_sem,
+        device_id={"expert": peer},
+        device_id_type=pl.DeviceIdType.MESH,
+    )
+
+
+def slice_copy(source, target, sends, recvs, base, member, mask, start, count):
+    rows, width = source.shape[0], target.shape[1]
+    partner = partner_of(member, mask)
+    return push(
+        source.at[:, pl.ds(pl.multiple_of(partner * width + start, 128), count)],
+        target.at[pl.ds(mask * rows, rows), pl.ds(start, count)],
+        sends, recvs, base + partner,
+    )
+
+
+def dispatch_kernel(
+    groups, capacity, outgoing, gate_up, master, targets,
+    hidden, master_in, goal_in,
+    arrived, group_send, group_recv, row_send, row_recv, unit_send, unit_recv,
+    state_send, state_recv,
+):
+    bf16, f32 = jnp.bfloat16, jnp.float32
+    here = lax.axis_index("expert")
+    me, member = here // GROUP, lax.rem(here, GROUP)
+    base = me * GROUP
+    units = gate_up.shape[1]
+    block = GROUP * capacity
+    greet(
+        [lax.rem(me + d, groups) * GROUP + member for d in range(1, groups)]
+        + [base + partner_of(member, mask) for mask in range(1, GROUP)]
+    )
+
+    def rows_of(group, part):
+        return pl.ds(pl.multiple_of(group * block + part * capacity, capacity), capacity)
+
+    def group_copy(d):
+        ahead = lax.rem(me + d, groups)
+        return push(
+            outgoing.at[pl.ds(pl.multiple_of(ahead * capacity, capacity), capacity)],
+            arrived.at[rows_of(me, 0)],
+            group_send.at[d - 1], group_recv.at[d - 1], ahead * GROUP + member,
+        )
+
+    def source_of(d):
+        return lax.rem(me + groups - d, groups)
+
+    def row_copy(d, mask):
+        group = source_of(d)
+        if mask == 3:
+            source, peer = arrived.at[rows_of(group, 2)], partner_of(member, 1)
+        elif d == 0:
+            source = outgoing.at[pl.ds(pl.multiple_of(me * capacity, capacity), capacity)]
+            peer = partner_of(member, mask)
+        else:
+            source, peer = arrived.at[rows_of(group, 0)], partner_of(member, mask)
+        return push(
+            source, arrived.at[rows_of(group, mask)],
+            row_send.at[d, mask - 1], row_recv.at[d, mask - 1], base + peer,
+        )
+
+    def unit_copy(d, mask, part):
+        group = source_of(d)
+        flip = 1 if mask == 3 else mask
+        origin = 2 if mask == 3 else 0
+        return push(
+            hidden.at[rows_of(group, part), pl.ds(origin * units, units)],
+            hidden.at[rows_of(group, part ^ flip), pl.ds(mask * units, units)],
+            unit_send.at[d, mask - 1, part], unit_recv.at[d, mask - 1, part],
+            base + partner_of(member, flip),
+        )
+
+    states = ((master, master_in), (targets, goal_in))
+
+    def state_copy(which, mask):
+        source, target = states[which]
+        return slice_copy(
+            source, target, state_send.at[which, mask - 1], state_recv.at[which, mask - 1],
+            base, member, mask, 0, target.shape[1],
+        )
+
+    order = sorted(range(1, groups), key=lambda d: min(d, groups - d))
+    for d in reversed(order):
+        group_copy(d).start()
+    row_copy(0, 2).start()
+    row_copy(0, 1).start()
+    for mask in (2, 3, 1):
+        state_copy(0, mask).start()
+    mine = pl.ds(pl.multiple_of(me * capacity, capacity), capacity)
+    arrived[rows_of(me, 0)] = outgoing[mine]
+    for source, target in states:
+        rows, width = source.shape[0], target.shape[1]
+        target[pl.ds(0, rows)] = source[:, pl.ds(pl.multiple_of(member * width, 128), width)]
+
+    def relay(d):
+        row_copy(d, 2).wait_recv()
+        row_copy(d, 3).start()
+
+    def compute(d):
+        row_copy(d, 1).wait_recv()
+        row_copy(d, 3).wait_recv()
+        span = pl.ds(pl.multiple_of(source_of(d) * block, block), block)
+        acts = [
+            lax.dot_general(
+                arrived[span], gate_up[i], (((1,), (1,)), ((), ())), preferred_element_type=f32
+            )
+            for i in range(2)
+        ]
+        gated = acts[0] / (1.0 + jnp.exp(-acts[0])) * acts[1]
+        hidden[span, pl.ds(0, units)] = gated.astype(bf16)
+        for mask in (2, 1):
+            for part in range(GROUP):
+                unit_copy(d, mask, part).start()
+
+    chain = [0] + order
+    for d in order:
+        group_copy(d).wait_recv()
+        row_copy(d, 2).start()
+        row_copy(d, 1).start()
+    for mask in (2, 3, 1):
+        state_copy(1, mask).start()
+    for position, d in enumerate(chain):
+        relay(d)
+        if position:
+            compute(chain[position - 1])
+    compute(chain[-1])
+    for d in chain:
+        for part in range(GROUP):
+            unit_copy(d, 2, part).wait_recv()
+        for part in range(GROUP):
+            unit_copy(d, 3, part).start()
+    for d in chain:
+        for part in range(GROUP):
+            unit_copy(d, 1, part).wait_recv()
+            unit_copy(d, 3, part).wait_recv()
+    for which in range(2):
+        for mask in range(1, GROUP):
+            state_copy(which, mask).wait()
+    for d in order:
+        group_copy(d).wait_send()
+    for d in chain:
+        for mask in range(1, GROUP):
+            row_copy(d, mask).wait_send()
+            for part in range(GROUP):
+                unit_copy(d, mask, part).wait_send()
+
+
+def dispatch(groups, capacity, outgoing, gate_up, master, targets):
+    bf16 = jnp.bfloat16
+    units, feat_width = master.shape
+    width = feat_width // GROUP
+    rows = groups * GROUP * capacity
+    spec = pl.BlockSpec(memory_space=pltpu.VMEM)
+    pair = lambda *shape: [pltpu.SemaphoreType.DMA(shape)] * 2
+    return pl.pallas_call(
+        functools.partial(dispatch_kernel, groups, capacity),
+        out_shape=[
+            jax.ShapeDtypeStruct((rows, GROUP * units), bf16),
+            jax.ShapeDtypeStruct((GROUP * units, width), bf16),
+            jax.ShapeDtypeStruct((GROUP * targets.shape[0], width), bf16),
+        ],
+        in_specs=[spec] * 4,
+        out_specs=[spec] * 3,
+        scratch_shapes=[
+            pltpu.VMEM((rows, feat_width), bf16),
+            *pair(groups - 1), *pair(groups, 3), *pair(groups, 3, GROUP), *pair(2, 3),
+        ],
+        compiler_params=pltpu.CompilerParams(
+            collective_id=1, has_side_effects=True, vmem_limit_bytes=60 * 2**20
+        ),
+    )(outgoing, gate_up, master, targets)
+
+
 def member_gather(block, axis):
     across = flipped(block, 2)
     near = flipped(block, 1)
     far = flipped(across, 1)
     return jnp.concatenate([block, near, across, far], axis=axis)
-
-
-def feature_slice(block, index, width):
-    return lax.dynamic_slice_in_dim(block, index * width, width, axis=1)
-
-
-def to_slices(block, member):
-    width = block.shape[1] // GROUP
-    pieces = [feature_slice(block, member, width)]
-    for mask in range(1, GROUP):
-        pieces.append(flipped(feature_slice(block, member ^ mask, width), mask))
-    return jnp.stack(pieces)
 
 
 def to_rows(block, member):
@@ -49,14 +229,6 @@
     return jnp.concatenate(pieces, axis=1)
 
 
-def over_groups(block):
-    groups = block.shape[0]
-    lists = [[g * GROUP + m for g in range(groups)] for m in range(GROUP)]
-    return lax.all_to_all(
-        block, "expert", split_axis=0, concat_axis=0, tiled=True, axis_index_groups=lists
-    )
-
-
 CHUNKS = 2
 
 
@@ -64,7 +236,7 @@
     groups, block, hidden, hidden_t, picks, picks_t, weights, goal, master, first, second,
     moved_out, first_out,
     sum_out, sum_in, grad_out, grad_in, values, master_two, first_two, second_two, moved_one,
-    send_sems, recv_sems,
+    first_in, second_in, send_sems, recv_sems, state_send, state_recv,
 ):
     bf16, f32 = jnp.bfloat16, jnp.float32
     here = lax.axis_index("expert")
@@ -76,13 +248,19 @@
     unit_tile = units // GROUP
     tok_tile = tokens // GROUP
 
-    barrier = pltpu.get_barrier_semaphore()
-    for d in range(1, groups):
-        peer = lax.rem(me + d, groups) * GROUP + member
-        pl.semaphore_signal(
-            barrier, inc=1, device_id={"expert": peer}, device_id_type=pl.DeviceIdType.MESH
-        )
-    pl.semaphore_wait(barrier, groups - 1)
+    base = me * GROUP
+    greet(
+        [lax.rem(me + d, groups) * GROUP + member for d in range(1, groups)]
+        + [base + partner_of(member, mask) for mask in range(1, GROUP)]
+    )
+    states = ((first, first_in), (second, second_in))
+
+    def state_copy(which, chunk, mask):
+        source, target = states[which]
+        return slice_copy(
+            source, target, state_send.at[which, chunk, mask - 1],
+            state_recv.at[which, chunk, mask - 1], base, member, mask, chunk * part, part,
+        )
 
     def rows_of(group):
         return pl.ds(pl.multiple_of(group * block, block), block)
@@ -145,6 +323,10 @@
 
     def update(step, chunk):
         arrive(grad_out, grad_in, 2 * step + 1, chunk)
+        if step == 0:
+            for which in range(2):
+                for mask in range(1, GROUP):
+                    state_copy(which, chunk, mask).wait()
         count = step + 1
         first_fix = 1.0 - 0.9 ** (prior_steps + count)
         second_fix = 1.0 - 0.999 ** (prior_steps + count)
@@ -156,8 +338,8 @@
             gradient = jnp.dot(
                 hidden_t[span], grad_in[step, chunk], preferred_element_type=f32
             )
-            one = (first if step == 0 else first_two)[span, cols].astype(f32)
-            two = (second if step == 0 else second_two)[span, cols].astype(f32)
+            one = (first_in if step == 0 else first_two)[span, cols]
+            two = (second_in if step == 0 else second_two)[span, cols]
             one = 0.9 * one + 0.1 * gradient
             two = 0.999 * two + 0.001 * gradient * gradient
             change = (one / first_fix) / (jnp.sqrt(two / second_fix) + epsilon)
@@ -172,7 +354,15 @@
                 first_out[span, cols] = one.astype(bf16)
 
     for chunk in range(CHUNKS):
+        for which in range(2):
+            for mask in (2, 3, 1):
+                state_copy(which, chunk, mask).start()
+    for chunk in range(CHUNKS):
         forward(0, chunk)
+    for source, target in states:
+        target[pl.ds(0, source.shape[0])] = source[
+            :, pl.ds(pl.multiple_of(member * width, 128), width)
+        ]
     for step in range(2):
         for chunk in range(CHUNKS):
             residuals(step, chunk)
@@ -204,8 +394,9 @@
             travel, travel, travel, travel,
             pltpu.VMEM((picks_t.shape[1], width // CHUNKS), bf16),
             pltpu.VMEM((units, width), bf16),
-            state, state, state,
+            state, state, state, state, state,
             sems, sems,
+            pltpu.SemaphoreType.DMA((2, CHUNKS, 3)), pltpu.SemaphoreType.DMA((2, CHUNKS, 3)),
         ],
         compiler_params=pltpu.CompilerParams(
             collective_id=0, has_side_effects=True, vmem_limit_bytes=60 * 2**20
@@ -222,6 +413,7 @@
     groups = devices // GROUP
     experts = expert_home.shape[0]
     capacity = (5 * tok_rows * top_count * GROUP + 4 * devices - 1) // (4 * devices)
+    capacity = -(-capacity // 16) * 16
     slot_rows = groups * capacity
     bf16, f32 = jnp.bfloat16, jnp.float32
 
@@ -237,13 +429,13 @@
         pick_own = pick_own | (row_ids[:, None] == slot_dest[:, k][None, :])
     outgoing = jnp.dot(
         pick_own.astype(bf16), tokens, preferred_element_type=f32
-    ).astype(bf16).reshape(groups, capacity, feat_width)
+    ).astype(bf16)
 
     plan = member_gather(
         jnp.stack([slot_dest.T, gate_ints.T], axis=1)[None], 0
     )
     all_dest, all_gates = plan[:, :, 0], plan[:, :, 1]
-    block = -(-GROUP * capacity // 16) * 16
+    block = GROUP * capacity
     rows = groups * block
     offsets = (jnp.arange(GROUP, dtype=jnp.int32) * capacity)[:, None, None]
     all_dest = all_dest // capacity * block + all_dest % capacity + offsets
@@ -254,49 +446,13 @@
     picks = (by_choice[:, :, None] == buffer_ids).astype(bf16)
     picks_t = (buffer_ids[:, None] == by_choice.reshape(-1)).astype(bf16)
 
-    arrived = member_gather(over_groups(outgoing), 1)
-    arrived = jnp.pad(arrived, ((0, 0), (0, block - GROUP * capacity), (0, 0)))
-    arrived = arrived.reshape(rows, feat_width)
-
-    master = to_slices(down_master.astype(bf16), member)
-    goal = to_slices(targets, member)
-    moment_one = to_slices(moment1.astype(bf16), member)
-    moment_two = to_slices(moment2.astype(bf16), member)
-    units = master.shape[1]
-    flat = (GROUP * units, width)
-    master = master.reshape(flat)
-    moment_one = moment_one.reshape(flat)
-    moment_two = moment_two.reshape(flat)
-    goal = goal.reshape(GROUP * tok_rows, width)
-
-    gate_acts = lax.dot_general(
-        arrived, gate_up[0], (((1,), (1,)), ((), ())), preferred_element_type=f32
-    )
-    up_acts = lax.dot_general(
-        arrived, gate_up[1], (((1,), (1,)), ((), ())), preferred_element_type=f32
-    )
-    def reordered(piece, mask):
-        piece = piece.reshape(groups, block, -1)
-        parts = [
-            piece[:, (i ^ mask) * capacity : ((i ^ mask) + 1) * capacity] for i in range(GROUP)
-        ]
-        parts.append(piece[:, GROUP * capacity :])
-        return jnp.concatenate(parts, axis=1).reshape(rows, -1)
-
-    own_hidden = (jax.nn.silu(gate_acts) * up_acts).astype(bf16)
-    across = flipped(own_hidden, 2)
-    hiddens = [own_hidden, flipped(own_hidden, 1), across, flipped(across, 1)]
-    hidden = jnp.concatenate(
-        [
-            reordered(piece, mask)
-            for mask, piece in enumerate(hiddens)
-        ],
-        axis=1,
-    )
-
+    hidden, master, goal = dispatch(
+        groups, capacity, outgoing, gate_up, down_master.astype(bf16), targets
+    )
+    units, width = down_master.shape[0], feat_width // GROUP
     moved, moment_one = refit(
         groups, block, hidden, hidden.T, picks, picks_t, weights, goal,
-        master, moment_one, moment_two,
+        master, moment1, moment2,
     )
     shape = (GROUP, units, width)
     return (

time: 298 us -> 258 us (0.87)
  Pallas kernels: 126 us -> 209 us
  waiting for transfers between devices: 66.3 us -> 17 us
  blocking collectives: 33.2 us -> 0 us
  starting transfers between devices: 24.3 us -> 8.33 us
  other arithmetic: 28.6 us -> 13.1 us
  local copies, waits for them, and re-layouts: 14.1 us -> 8.72 us
    pallas_call x0 -> x1, Pallas kernels: none -> 75.6 us  [dispatch(): pl.pallas_call(functools.partial(dispatch_kernel, groups, capacity), out_...]
    ppermute x27 -> x9, waiting for transfers between devices: 66.3 us -> 17 us  [flipped(): return lax.ppermute(block, 'expert', [(i, i ^ mask) for i in range(count)])]
    all_to_all x1 -> x0, blocking collectives: 33.2 us -> none  [over_groups(): lax.all_to_all(block, 'expert', split_axis=0, concat_axis=0, tiled=True,...]
    ppermute x27 -> x9, starting transfers between devices: 24.3 us -> 8.33 us  [flipped(): return lax.ppermute(block, 'expert', [(i, i ^ mask) for i in range(count)])]
    another operation x6 -> x2, other arithmetic: 8.47 us -> 1.26 us  [the longest x4 7.21 us: to_slices(): return jnp.stack(pieces)]
    pallas_call x1, Pallas kernels: 126 us -> 133 us  [refit(): pl.pallas_call(functools.partial(rounds_kernel, groups, block), out_shape...]
    concatenate x2 -> x1, other arithmetic: 5.13 us -> 0.01 us  [member_gather(): return jnp.concatenate([block, near, across, far], axis=axis)]
    pallas_call x0 -> x1, local copies, waits for them, and re-layouts: none -> 4.41 us  [dispatch(): pl.pallas_call(functools.partial(dispatch_kernel, groups, capacity), out_...]
  transfers between devices with their start and end apart: 27 -> 9, of which waited for: 10 -> 4; matrix products, arithmetic and copies ran while one was open for 11% -> 4% of each run, Pallas kernels for 0% -> 29%
where the time goes in v3:
time: 258 us
  Pallas kernels  209 us (81%)
  waiting for transfers between devices  17 us (7%)
  other arithmetic  13.1 us (5%)
  local copies, waits for them, and re-layouts  8.72 us (3%)
  starting transfers between devices  8.33 us (3%)
    pallas_call x1, Pallas kernels, refit(): pl.pallas_call(functools.partial(rounds_kernel, groups, block), out_shape...  133 us
    pallas_call x1, Pallas kernels, dispatch(): pl.pallas_call(functools.partial(dispatch_kernel, groups, capacity), out_...  75.6 us
    ppermute x9, waiting for transfers between devices, flipped(): return lax.ppermute(block, 'expert', [(i, i ^ mask) for i in range(count)])  17 us
    ppermute x9, starting transfers between devices, flipped(): return lax.ppermute(block, 'expert', [(i, i ^ mask) for i in range(count)])  8.33 us
  transfers between devices with their start and end apart: 9, of which 4 were waited for; matrix products, arithmetic and copies ran while one was open for 4% of the time, Pallas kernels for 29%

profile of v3, /device:TPU:11, one launch (start us, length us, event | category | flops | bytes accessed | tf_op | source)
XLA Modules:
  0.0 258.1 jit_solution(14430590610703601276)
XLA Ops:
  0.7 0.9 copy.44
  1.6 0.1 eq.104
  1.7 0.1 eq.100
  1.9 1.2 reduce-window.6
  3.5 0.7 select_reduce_fusion
  4.3 0.1 add.31
  4.5 0.7 pad_add_fusion.1
  5.2 1.2 collective-permute-start.1
  6.4 1.0 collective-permute-start
  7.4 0.2 slice_reduce_fusion.1
  7.6 1.6 convolution_convert_fusion.outgoing
  9.1 0.3 collective-permute-start.2
  9.4 1.1 convert_element_type.43.master
  10.6 75.6 %shard_map.104 = (bf16[1280,1024]{1,0:T(8,128)(2,1)}, bf16[1024,512]{1,0:T(8,128)(2,1)}, bf16[512,512]{1,0:T(8,128)(2,1)}) custom-call(bf16[320,2048]{1,0:T(8,128)(2,1)} %convolution_convert_fusion.outgoing, bf16[2,256,2048]{2,1,0:T(8,128)(2,1)} %gate_up.1, bf16[256,2048]{1,0:T(8,128)(2,1)} %convert_element_type.43.master, bf16[128,2048]{1,0:T(8,128)(2,1)} %targets.1), custom_call_target="tpu_custom_call" | custom-call | tf_op jit(solution)/shard_map/pallas_call | solution.py:197
  86.1 4.4 %copy.48 = bf16[1280,1024]{0,1:T(8,128)(2,1)} copy(bf16[1280,1024]{1,0:T(8,128)(2,1)} %get-tuple-element.7.hidden) | data formatting | bytes 5242880 | tf_op jit(solution)/shard_map/pallas_call | solution.py:197
  90.7 2.0 fusion.picks
  92.7 2.7 %fusion.1.picks_t = bf16[1280,1024]{1,0:T(8,128)(2,1)} fusion(s32[1024]{0:T(1024)S(1)} %bitcast.104), kind=kLoop, calls=%fused_computation.3 | loop fusion | flops 2621440 | bytes 2625536 | tf_op jit(solution)/shard_map/convert_element_type | solution.py:447
  95.5 1.1 div.28.weights
  96.6 133.0 %shard_map.105 = (bf16[1024,512]{1,0:T(8,128)(2,1)}, bf16[1024,512]{1,0:T(8,128)(2,1)}) custom-call(bf16[1280,1024]{1,0:T(8,128)(2,1)} %get-tuple-element.7.hidden, bf16[1024,1280]{1,0:T(8,128)(2,1)} %bitcast.102, bf16[2,512,1280]{2,1,0:T(8,128)(2,1)} %fusion.picks, bf16[1280,1024]{1,0:T(8,128)(2,1)} %fusion.1.picks_t, f32[2,512,1]{2,1,0:T(8,128)} %div.28.weights, ...), custom_call_target="tpu_custom_call" | custom-call | tf_op jit(solution)/shard_map/pallas_call | solution.py:388
  229.6 1.2 fusion.19
  231.0 2.5 collective-permute-start.7
  233.5 0.5 collective-permute-start.3
  234.0 1.5 collective-permute-start.4
  235.4 3.9 %collective-permute-done.6 = bf16[256,512]{1,0:T(8,128)(2,1)S(1)} collective-permute-done((bf16[256,512]{1,0:T(8,128)(2,1)S(1)}, bf16[256,512]{1,0:T(8,128)(2,1)S(1)}, u32[]{:S(2)}, u32[]{:S(2)}) %collective-permute-start.6) | collective-permute-done | bytes 262176 | tf_op jit(solution)/shard_map/ppermute | solution.py:21
  239.4 1.3 collective-permute-start.5
  240.7 4.9 %collective-permute-done.7 = bf16[256,512]{1,0:T(8,128)(2,1)S(1)} collective-permute-done((bf16[256,512]{1,0:T(8,128)(2,1)S(1)}, bf16[256,512]{1,0:T(8,128)(2,1)S(1)}, u32[]{:S(2)}, u32[]{:S(2)}) %collective-permute-start.7) | collective-permute-done | bytes 262176 | tf_op jit(solution)/shard_map/ppermute | solution.py:21
  245.6 1.0 broadcast_select_fusion.11
  246.7 1.6 maximum_convert_fusion.1
  248.2 2.4 collective-permute-done.3
  250.6 5.8 %collective-permute-done.4 = bf16[256,512]{1,0:T(8,128)(2,1)S(1)} collective-permute-done((bf16[256,512]{1,0:T(8,128)(2,1)S(1)}, bf16[256,512]{1,0:T(8,128)(2,1)S(1)}, u32[]{:S(2)}, u32[]{:S(2)}) %collective-permute-start.4) | collective-permute-done | bytes 262176 | tf_op jit(solution)/shard_map/ppermute | solution.py:21
  256.4 0.1 broadcast_select_fusion.15
  256.5 1.6 maximum_convert_fusion
  (29 shorter events, 0.8 us)
Async XLA Ops:
  0.6 6.9 %copy-start = (bf16[128,2048]{1,0:T(8,128)(2,1)S(1)}, bf16[128,2048]{1,0:T(8,128)(2,1)}, u32[]{:S(2)}) copy-start(bf16[128,2048]{1,0:T(8,128)(2,1)} %param.9) | copy-start | bytes 1572868
  0.6 8.8 %copy-start.1 = (f32[256,2048]{1,0:T(8,128)S(1)}, f32[256,2048]{1,0:T(8,128)}, u32[]{:S(2)}) copy-start(f32[256,2048]{1,0:T(8,128)} %param.15) | copy-start | bytes 6291460
  5.2 3.9 %collective-permute-start.1 = (s32[1,2,2,128]{3,2,1,0:T(2,128)S(1)}, s32[1,2,2,128]{3,2,1,0:T(2,128)S(1)}, u32[]{:S(2)}, u32[]{:S(2)}) collective-permute-start(s32[1,2,2,128]{3,2,1,0:T(2,128)S(1)} %get-tuple-element.31), channel_id=1, source_target_pairs={{0,2},{1,3},{2,0},{3,1},{4,6},{5,7},{6,4},{7,5},{8,10},{9,11},{10,... | collective-permute-start | bytes 6152 | tf_op jit(solution)/shard_map/ppermute | solution.py:21
  6.4 84.1 %collective-permute-start = (s32[1,2,2,128]{3,2,1,0:T(2,128)S(1)}, s32[1,2,2,128]{3,2,1,0:T(2,128)S(1)}, u32[]{:S(2)}, u32[]{:S(2)}) collective-permute-start(s32[1,2,2,128]{3,2,1,0:T(2,128)S(1)} %get-tuple-element.31), channel_id=1, source_target_pairs={{0,1},{1,0},{2,3},{3,2},{4,5},{5,4},{6,7},{7,6},{8,9},{9,8},{10,11... | collective-permute-start | bytes 6152 | tf_op jit(solution)/shard_map/ppermute | solution.py:21
  9.1 81.4 %collective-permute-start.2 = (s32[1,2,2,128]{3,2,1,0:T(2,128)S(1)}, s32[1,2,2,128]{3,2,1,0:T(2,128)S(1)}, u32[]{:S(2)}, u32[]{:S(2)}) collective-permute-start(s32[1,2,2,128]{3,2,1,0:T(2,128)S(1)} %collective-permute-done.1), channel_id=1, source_target_pairs={{0,1},{1,0},{2,3},{3,2},{4,5},{5,4},{6,7},{7,6},{8,9},{9,8},{10,11... | collective-permute-start | bytes 6152 | tf_op jit(solution)/shard_map/ppermute | solution.py:21
  229.6 3.8 %copy-start.2 = (bf16[1024,512]{1,0:T(8,128)(2,1)S(1)}, bf16[1024,512]{1,0:T(8,128)(2,1)}, u32[]{:S(2)}) copy-start(bf16[1024,512]{1,0:T(8,128)(2,1)} %get-tuple-element.10) | copy-start | bytes 3145732
  230.9 8.5 %collective-permute-start.6 = (bf16[256,512]{1,0:T(8,128)(2,1)S(1)}, bf16[256,512]{1,0:T(8,128)(2,1)S(1)}, u32[]{:S(2)}, u32[]{:S(2)}) collective-permute-start(bf16[256,512]{1,0:T(8,128)(2,1)S(1)} %get-tuple-element.26), channel_id=1, source_target_pairs={{0,3},{1,2},{2,1},{3,0},{4,7},{5,6},{6,5},{7,4},{8,11},{9,10},{10,... | collective-permute-start | bytes 786440 | tf_op jit(solution)/shard_map/ppermute | solution.py:21
  231.0 14.7 %collective-permute-start.7 = (bf16[256,512]{1,0:T(8,128)(2,1)S(1)}, bf16[256,512]{1,0:T(8,128)(2,1)S(1)}, u32[]{:S(2)}, u32[]{:S(2)}) collective-permute-start(bf16[256,512]{1,0:T(8,128)(2,1)S(1)} %get-tuple-element.25), channel_id=1, source_target_pairs={{0,2},{1,3},{2,0},{3,1},{4,6},{5,7},{6,4},{7,5},{8,10},{9,11},{10,... | collective-permute-start | bytes 786440 | tf_op jit(solution)/shard_map/ppermute | solution.py:21
  233.5 12.2 %collective-permute-start.8 = (bf16[256,512]{1,0:T(8,128)(2,1)S(1)}, bf16[256,512]{1,0:T(8,128)(2,1)S(1)}, u32[]{:S(2)}, u32[]{:S(2)}) collective-permute-start(bf16[256,512]{1,0:T(8,128)(2,1)S(1)} %get-tuple-element.24), channel_id=1, source_target_pairs={{0,1},{1,0},{2,3},{3,2},{4,5},{5,4},{6,7},{7,6},{8,9},{9,8},{10,11... | collective-permute-start | bytes 786440 | tf_op jit(solution)/shard_map/ppermute | solution.py:21
  233.5 17.1 %collective-permute-start.3 = (bf16[256,512]{1,0:T(8,128)(2,1)S(1)}, bf16[256,512]{1,0:T(8,128)(2,1)S(1)}, u32[]{:S(2)}, u32[]{:S(2)}) collective-permute-start(bf16[256,512]{1,0:T(8,128)(2,1)S(1)} %get-tuple-element.29), channel_id=1, source_target_pairs={{0,3},{1,2},{2,1},{3,0},{4,7},{5,6},{6,5},{7,4},{8,11},{9,10},{10,... | collective-permute-start | bytes 786440 | tf_op jit(solution)/shard_map/ppermute | solution.py:21
  234.0 22.4 %collective-permute-start.4 = (bf16[256,512]{1,0:T(8,128)(2,1)S(1)}, bf16[256,512]{1,0:T(8,128)(2,1)S(1)}, u32[]{:S(2)}, u32[]{:S(2)}) collective-permute-start(bf16[256,512]{1,0:T(8,128)(2,1)S(1)} %get-tuple-element.28), channel_id=1, source_target_pairs={{0,2},{1,3},{2,0},{3,1},{4,6},{5,7},{6,4},{7,5},{8,10},{9,11},{10,... | collective-permute-start | bytes 786440 | tf_op jit(solution)/shard_map/ppermute | solution.py:21
  239.4 17.0 %collective-permute-start.5 = (bf16[256,512]{1,0:T(8,128)(2,1)S(1)}, bf16[256,512]{1,0:T(8,128)(2,1)S(1)}, u32[]{:S(2)}, u32[]{:S(2)}) collective-permute-start(bf16[256,512]{1,0:T(8,128)(2,1)S(1)} %get-tuple-element.27), channel_id=1, source_target_pairs={{0,1},{1,0},{2,3},{3,2},{4,5},{5,4},{6,7},{7,6},{8,9},{9,8},{10,11... | collective-permute-start | bytes 786440 | tf_op jit(solution)/shard_map/ppermute | solution.py:21

commit v4 on v3

--- a/solution.py
+++ b/solution.py
@@ -220,23 +220,15 @@
     return jnp.concatenate([block, near, across, far], axis=axis)
 
 
-def to_rows(block, member):
-    pieces = [block[0]] + [flipped(block[mask], mask) for mask in range(1, GROUP)]
-    for bit in range(GROUP.bit_length() - 1):
-        upper = (member >> bit & 1) == 1
-        step = 1 << bit
-        pieces = [jnp.where(upper, pieces[i ^ step], pieces[i]) for i in range(GROUP)]
-    return jnp.concatenate(pieces, axis=1)
-
-
 CHUNKS = 2
 
 
 def rounds_kernel(
-    groups, block, hidden, hidden_t, picks, picks_t, weights, goal, master, first, second,
-    moved_out, first_out,
+    groups, block, hidden, dest, dest_t, weights, goal, master, first, second,
+    moved_rows, first_rows,
+    moved_out, first_out, picks, picks_t,
     sum_out, sum_in, grad_out, grad_in, values, master_two, first_two, second_two, moved_one,
-    first_in, second_in, send_sems, recv_sems, state_send, state_recv,
+    first_in, second_in, send_sems, recv_sems, state_send, state_recv, out_send, out_recv,
 ):
     bf16, f32 = jnp.bfloat16, jnp.float32
     here = lax.axis_index("expert")
@@ -335,8 +327,9 @@
         @pl.loop(0, GROUP)
         def _(tile):
             span = pl.ds(pl.multiple_of(tile * unit_tile, unit_tile), unit_tile)
-            gradient = jnp.dot(
-                hidden_t[span], grad_in[step, chunk], preferred_element_type=f32
+            gradient = lax.dot_general(
+                hidden[:, span], grad_in[step, chunk], (((0,), (0,)), ((), ())),
+                preferred_element_type=f32,
             )
             one = (first_in if step == 0 else first_two)[span, cols]
             two = (second_in if step == 0 else second_two)[span, cols]
@@ -353,12 +346,48 @@
                 moved_out[span, cols] = (moved_one[span, cols] + change).astype(bf16)
                 first_out[span, cols] = one.astype(bf16)
 
+    results = ((moved_out, moved_rows), (first_out, first_rows))
+    own_units = first.shape[0]
+
+    def out_columns(chunk):
+        return pl.ds(pl.multiple_of(member * width + chunk * part, 128), part)
+
+    def out_copy(which, chunk, mask):
+        source, target = results[which]
+        return push(
+            source.at[pl.ds(mask * own_units, own_units), columns(chunk)],
+            target.at[:, out_columns(chunk)],
+            out_send.at[which, chunk, mask - 1], out_recv.at[which, chunk, mask - 1],
+            base + partner_of(member, mask),
+        )
+
+    def hand_out(chunk):
+        for mask in (2, 3, 1):
+            for which in range(2):
+                out_copy(which, chunk, mask).start()
+        for source, target in results:
+            target[:, out_columns(chunk)] = source[pl.ds(0, own_units), columns(chunk)]
+
     for chunk in range(CHUNKS):
         for which in range(2):
             for mask in (2, 3, 1):
                 state_copy(which, chunk, mask).start()
     for chunk in range(CHUNKS):
         forward(0, chunk)
+    slots = lax.broadcasted_iota(jnp.int32, (tok_tile, hidden.shape[0]), 1)
+    for k in range(top_count):
+
+        @pl.loop(0, GROUP)
+        def _(tile):
+            span = pl.ds(pl.multiple_of(tile * tok_tile, tok_tile), tok_tile)
+            picks[k, span] = jnp.where(dest[k, span] == slots, 1.0, 0.0).astype(bf16)
+
+    @pl.loop(0, hidden.shape[0] // block)
+    def _(tile):
+        span = pl.ds(pl.multiple_of(tile * block, block), block)
+        slot = lax.broadcasted_iota(jnp.int32, (block, dest_t.shape[1]), 0) + tile * block
+        picks_t[span] = jnp.where(dest_t[...] == slot, 1.0, 0.0).astype(bf16)
+
     for source, target in states:
         target[pl.ds(0, source.shape[0])] = source[
             :, pl.ds(pl.multiple_of(member * width, 128), width)
@@ -370,6 +399,12 @@
             update(step, chunk)
             if step == 0:
                 forward(1, chunk)
+            else:
+                hand_out(chunk)
+    for chunk in range(CHUNKS):
+        for which in range(2):
+            for mask in range(1, GROUP):
+                out_copy(which, chunk, mask).wait()
     for phase in range(4):
         source, target = ((sum_out, sum_in), (grad_out, grad_in))[phase % 2]
         for chunk in range(CHUNKS):
@@ -377,7 +412,7 @@
                 copy_to(source, target, phase, chunk, d).wait_send()
 
 
-def refit(groups, block, hidden, hidden_t, picks, picks_t, weights, goal, master, first, second):
+def refit(groups, block, hidden, dest, dest_t, weights, goal, master, first, second):
     bf16, f32 = jnp.bfloat16, jnp.float32
     units, width = master.shape
     rows = hidden.shape[0]
@@ -387,21 +422,24 @@
     spec = pl.BlockSpec(memory_space=pltpu.VMEM)
     return pl.pallas_call(
         functools.partial(rounds_kernel, groups, block),
-        out_shape=[jax.ShapeDtypeStruct((units, width), bf16)] * 2,
-        in_specs=[spec] * 9,
+        out_shape=[jax.ShapeDtypeStruct(first.shape, bf16)] * 2,
+        in_specs=[spec] * 8,
         out_specs=[spec] * 2,
         scratch_shapes=[
+            pltpu.VMEM((units, width), bf16), pltpu.VMEM((units, width), bf16),
+            pltpu.VMEM((dest.shape[0], dest.shape[1], rows), bf16),
+            pltpu.VMEM((rows, dest_t.shape[1]), bf16),
             travel, travel, travel, travel,
-            pltpu.VMEM((picks_t.shape[1], width // CHUNKS), bf16),
+            pltpu.VMEM((dest_t.shape[1], width // CHUNKS), bf16),
             pltpu.VMEM((units, width), bf16),
             state, state, state, state, state,
             sems, sems,
-            pltpu.SemaphoreType.DMA((2, CHUNKS, 3)), pltpu.SemaphoreType.DMA((2, CHUNKS, 3)),
+            *[pltpu.SemaphoreType.DMA((2, CHUNKS, 3))] * 4,
         ],
         compiler_params=pltpu.CompilerParams(
             collective_id=0, has_side_effects=True, vmem_limit_bytes=60 * 2**20
         ),
-    )(hidden, hidden_t, picks, picks_t, weights, goal, master, first, second)
+    )(hidden, dest, dest_t, weights, goal, master, first, second)
 
 
 def shards(tokens, targets, routes, gate_ints, expert_home, gate_up, down_master, moment1, moment2):
@@ -442,23 +480,15 @@
     by_choice = all_dest.transpose(1, 0, 2).reshape(top_count, GROUP * tok_rows)
     weights = all_gates.transpose(1, 0, 2).reshape(top_count, GROUP * tok_rows, 1)
     weights = weights.astype(f32) / 4096.0
-    buffer_ids = jnp.arange(rows, dtype=jnp.int32)
-    picks = (by_choice[:, :, None] == buffer_ids).astype(bf16)
-    picks_t = (buffer_ids[:, None] == by_choice.reshape(-1)).astype(bf16)
 
     hidden, master, goal = dispatch(
         groups, capacity, outgoing, gate_up, down_master.astype(bf16), targets
     )
-    units, width = down_master.shape[0], feat_width // GROUP
     moved, moment_one = refit(
-        groups, block, hidden, hidden.T, picks, picks_t, weights, goal,
+        groups, block, hidden, by_choice[:, :, None], by_choice.reshape(1, -1), weights, goal,
         master, moment1, moment2,
     )
-    shape = (GROUP, units, width)
-    return (
-        to_rows(moved.reshape(shape), member).astype(f32),
-        to_rows(moment_one.reshape(shape), member).astype(f32),
-    )
+    return moved.astype(f32), moment_one.astype(f32)
 
 
 def solution(mesh):

time: 258 us -> 240 us (0.930); the launches traced: 258 us -> 235 us
  waiting for transfers between devices: 17 us -> 0.01 us
  Pallas kernels: 209 us -> 217 us
  starting transfers between devices: 8.33 us -> 2.52 us
  local copies, waits for them, and re-layouts: 8.72 us -> 4.15 us
  other arithmetic: 13.1 us -> 9.11 us
    ppermute x9 -> x3, waiting for transfers between devices: 17 us -> 0.01 us  [flipped(): return lax.ppermute(block, 'expert', [(i, i ^ mask) for i in range(count)])]
    pallas_call x1, Pallas kernels: 133 us -> 142 us  [refit(): pl.pallas_call(functools.partial(rounds_kernel, groups, block), out_shape...]
    ppermute x9 -> x3, starting transfers between devices: 8.33 us -> 2.52 us  [flipped(): return lax.ppermute(block, 'expert', [(i, i ^ mask) for i in range(count)])]
    pallas_call x1 -> x0, local copies, waits for them, and re-layouts: 4.41 us -> none  [dispatch(): pl.pallas_call(functools.partial(dispatch_kernel, groups, capacity), out_...]
    convert_element_type x4 -> x2, other arithmetic: 7.86 us -> 4.43 us  [shards(): return (moved.astype(f32), moment_one.astype(f32))]
  transfers between devices with their start and end apart: 9 -> 3, of which waited for: 4 -> 0; matrix products, arithmetic and copies ran while one was open for 4% -> 1% of each run, Pallas kernels for 29% -> 32%
where the time goes in v4:
time: 240 us; the launch traced here: 235 us
  Pallas kernels  217 us (90%)
  other arithmetic  9.11 us (4%)
  local copies, waits for them, and re-layouts  4.15 us (2%)
  starting transfers between devices  2.52 us (1%)
    pallas_call x1, Pallas kernels, refit(): pl.pallas_call(functools.partial(rounds_kernel, groups, block), out_shape...  142 us
    pallas_call x1, Pallas kernels, dispatch(): pl.pallas_call(functools.partial(dispatch_kernel, groups, capacity), out_...  75.5 us
  transfers between devices with their start and end apart: 3, of which 0 were waited for; matrix products, arithmetic and copies ran while one was open for 1% of the time, Pallas kernels for 32%

profile of v4, /device:TPU:11, one launch (start us, length us, event | category | flops | bytes accessed | tf_op | source)
XLA Modules:
  0.0 235.3 jit_solution(2596762531472860310)
XLA Ops:
  0.6 0.0 copy-start
  0.7 0.9 copy.45
  1.6 0.1 eq.58
  1.7 0.1 eq.62
  1.9 1.2 reduce-window.6
  3.1 0.1 slice.24
  3.2 0.1 copy.47
  3.3 0.1 copy.48
  3.4 0.1 add_bitcast_fusion
  3.5 0.7 select_reduce_fusion
  4.3 0.1 add.26
  4.4 0.1 copy.49
  4.5 0.7 pad_add_fusion.1
  5.2 1.2 collective-permute-start.1
  6.4 1.0 collective-permute-start
  7.4 0.2 slice_reduce_fusion.1
  7.5 0.0 copy-done
  7.6 1.6 convolution_convert_fusion.outgoing
  9.1 0.0 collective-permute-done.1
  9.1 0.3 collective-permute-start.2
  9.4 1.1 convert_element_type.37.master
  10.6 75.5 %shard_map.104 = (bf16[1280,1024]{1,0:T(8,128)(2,1)}, bf16[1024,512]{1,0:T(8,128)(2,1)}, bf16[512,512]{1,0:T(8,128)(2,1)}) custom-call(bf16[320,2048]{1,0:T(8,128)(2,1)} %convolution_convert_fusion.outgoing, bf16[2,256,2048]{2,1,0:T(8,128)(2,1)} %gate_up.1, bf16[256,2048]{1,0:T(8,128)(2,1)} %convert_element_type.37.master, bf16[128,2048]{1,0:T(8,128)(2,1)} %targets.1), custom_call_target="tpu_custom_call" | custom-call | tf_op jit(solution)/shard_map/pallas_call | solution.py:197
  86.1 0.0 collective-permute-done
  86.1 0.0 collective-permute-done.2
  86.1 0.1 fusion.18
  86.2 0.7 fusion.6
  86.9 1.1 broadcast_in_dim_reshape.5.dest
  88.0 1.1 div.28.weights
  89.2 141.7 %shard_map.105 = (bf16[256,2048]{1,0:T(8,128)(2,1)}, bf16[256,2048]{1,0:T(8,128)(2,1)}) custom-call(bf16[1280,1024]{1,0:T(8,128)(2,1)} %get-tuple-element.7.hidden, s32[2,512,1]{2,1,0:T(8,128)} %broadcast_in_dim_reshape.5.dest, s32[1,1024]{1,0:T(1,128)} %bitcast.98, f32[2,512,1]{2,1,0:T(8,128)} %div.28.weights, bf16[512,512]{1,0:T(8,128)(2,1)} %get-tuple-element.8.goal, ...), custom_call_target="tpu_custom_call" | custom-call | tf_op jit(solution)/shard_map/pallas_call | solution.py:423
  230.8 2.9 %convert_element_type.39 = f32[256,2048]{1,0:T(8,128)} convert(bf16[256,2048]{1,0:T(8,128)(2,1)} %get-tuple-element.10) | non-fusion elementwise | flops 524288 | bytes 3145728 | tf_op jit(solution)/shard_map/convert_element_type | solution.py:491
  233.7 0.0 copy-done.2
  233.7 1.6 convert_element_type.40
  (10 shorter events, 0.1 us)
Async XLA Ops:
  0.6 6.9 %copy-start = (bf16[128,2048]{1,0:T(8,128)(2,1)S(1)}, bf16[128,2048]{1,0:T(8,128)(2,1)}, u32[]{:S(2)}) copy-start(bf16[128,2048]{1,0:T(8,128)(2,1)} %param.9) | copy-start | bytes 1572868
  0.6 8.8 %copy-start.1 = (f32[256,2048]{1,0:T(8,128)S(1)}, f32[256,2048]{1,0:T(8,128)}, u32[]{:S(2)}) copy-start(f32[256,2048]{1,0:T(8,128)} %param.15) | copy-start | bytes 6291460
  5.2 3.9 %collective-permute-start.1 = (s32[1,2,2,128]{3,2,1,0:T(2,128)S(1)}, s32[1,2,2,128]{3,2,1,0:T(2,128)S(1)}, u32[]{:S(2)}, u32[]{:S(2)}) collective-permute-start(s32[1,2,2,128]{3,2,1,0:T(2,128)S(1)} %get-tuple-element.17), channel_id=1, source_target_pairs={{0,2},{1,3},{2,0},{3,1},{4,6},{5,7},{6,4},{7,5},{8,10},{9,11},{10,... | collective-permute-start | bytes 6152 | tf_op jit(solution)/shard_map/ppermute | solution.py:21
  6.4 79.7 %collective-permute-start = (s32[1,2,2,128]{3,2,1,0:T(2,128)S(1)}, s32[1,2,2,128]{3,2,1,0:T(2,128)S(1)}, u32[]{:S(2)}, u32[]{:S(2)}) collective-permute-start(s32[1,2,2,128]{3,2,1,0:T(2,128)S(1)} %get-tuple-element.17), channel_id=1, source_target_pairs={{0,1},{1,0},{2,3},{3,2},{4,5},{5,4},{6,7},{7,6},{8,9},{9,8},{10,11... | collective-permute-start | bytes 6152 | tf_op jit(solution)/shard_map/ppermute | solution.py:21
  9.1 77.0 %collective-permute-start.2 = (s32[1,2,2,128]{3,2,1,0:T(2,128)S(1)}, s32[1,2,2,128]{3,2,1,0:T(2,128)S(1)}, u32[]{:S(2)}, u32[]{:S(2)}) collective-permute-start(s32[1,2,2,128]{3,2,1,0:T(2,128)S(1)} %collective-permute-done.1), channel_id=1, source_target_pairs={{0,1},{1,0},{2,3},{3,2},{4,5},{5,4},{6,7},{7,6},{8,9},{9,8},{10,11... | collective-permute-start | bytes 6152 | tf_op jit(solution)/shard_map/ppermute | solution.py:21
  230.8 2.9 %copy-start.2 = (bf16[256,2048]{1,0:T(8,128)(2,1)S(1)}, bf16[256,2048]{1,0:T(8,128)(2,1)}, u32[]{:S(2)}) copy-start(bf16[256,2048]{1,0:T(8,128)(2,1)} %get-tuple-element.11) | copy-start | bytes 3145732
